TPU v7x, 256 devices: a whole 4x4x8 slice. The times are simulated.
256 devices in a mesh: gx: 64 (over z, y, core), gy: 4 (over x).
Axes of the slice: x: 4, y: 4, z: 8, core: 2. Of those that a mesh axis runs over, the one named last changes fastest.
Arguments:
- anomalies: float32 [131072, 1024], P(('gx', 'gy')), may hold values from -50 to 50
- obs_rows: int32 [64, 256], replicated, may hold values from 0 to 6143
- obs_var: float32 [64, 256], P('gx'), may hold values from 0.5 to 20
- taper_level: int32 [64, 3, 4], replicated, may hold values from 0 to 3
Outputs:
- posterior: float32 [131072, 1024], P(('gx', 'gy'))
All inputs are finite; a program needn't handle non-finite values.
Results may differ from a plain program's by a relative error of at most 0.035.
The roundings to bfloat16 on the way count: a program that leaves them out, or rounds other values in their place, can miss the bound.
Values may be sent and summed in bfloat16 or wider, within the bound.
No kernel may reach another device: no remote copies, remote signals or barrier semaphores. Data moves between devices by JAX's collectives and lax.ppermute only.
A program may use at most 64 MiB of HBM per device.

v0:
```python
import functools

import jax
import jax.numpy as jnp
from jax import lax
from jax.experimental import pallas as pl
from jax.experimental.pallas import tpu as pltpu
from jax.sharding import PartitionSpec as P

NCOL = 4
NS_STEPS = 12
AXES = ("gx", "gy")
VMEM_LIMIT = 20 << 20
INTERPRET = False
F32 = jnp.float32
BF16 = jnp.bfloat16


def kernel_call(body, out, args, name, flops, smem=(), scratch=()):
    whole = pl.BlockSpec(memory_space=pltpu.VMEM)
    scalar = pl.BlockSpec(memory_space=pltpu.SMEM)
    leaves = [*args, *jax.tree.leaves(out)]
    return pl.pallas_call(
        body,
        out_shape=out,
        in_specs=[scalar if n in smem else whole for n in range(len(args))],
        out_specs=jax.tree.map(lambda _: whole, out),
        scratch_shapes=scratch,
        name=name,
        interpret=INTERPRET,
        cost_estimate=pl.CostEstimate(
            flops=flops,
            bytes_accessed=sum(leaf.size * leaf.dtype.itemsize for leaf in leaves),
            transcendentals=0,
        ),
        compiler_params=pltpu.CompilerParams(vmem_limit_bytes=VMEM_LIMIT),
    )(*args)


def dot(left, right):
    return jnp.dot(left, right, preferred_element_type=F32)


def dot_nt(left, right):
    return lax.dot_general(
        left, right, (((1,), (1,)), ((), ())), preferred_element_type=F32
    )


def dot_tn(left, right):
    return lax.dot_general(
        left, right, (((0,), (0,)), ((), ())), preferred_element_type=F32
    )


def halves(value):
    high = value.astype(BF16)
    return high, (value - high.astype(F32)).astype(BF16)


def mat_prod(left, right):
    return dot(left[0], right[0]) + (dot(left[0], right[1]) + dot(left[1], right[0]))


def standing(col, colour, columns):
    offset = lax.rem(col + (NCOL - colour), NCOL)
    slot = jnp.where(offset == 1, 2, jnp.where(offset == 3, 0, 1))
    return slot, offset != 2, lax.rem(col - slot + 1 + columns, columns)


def pick_kernel(colours, state, obs, place, *refs):
    outs, scratch = refs[:-1], refs[-1]
    tiles = len(outs)
    tile_rows = state.shape[0]
    columns, size = obs.shape
    share = size // tiles
    col, tile = place[0, 0], place[0, 1]
    rest = state[...]
    parts = [rest.astype(BF16)]
    if outs[0].dtype == F32:
        rest = rest - parts[0].astype(F32)
        parts.append(rest.astype(BF16))
        parts.append((rest - parts[1].astype(F32)).astype(BF16))
    for n, colour in enumerate(colours):
        slot, active, batch = standing(col, colour, columns)
        first = jnp.where(active, (slot * tiles + tile) * tile_rows, -(1 << 20))
        local = obs[pl.ds(batch, 1), :] - first
        spots = lax.broadcasted_iota(jnp.int32, (tile_rows, size), 0)
        chosen = jnp.where(spots == local, 1.0, 0.0).astype(BF16)
        picked = dot_tn(chosen, parts[0])
        for part in parts[1:]:
            picked = picked + dot_tn(chosen, part)
        scratch[...] = picked.astype(scratch.dtype)
        for step, out in enumerate(outs):
            start = pl.multiple_of(lax.rem(tile + step, tiles) * share, share)
            out[n * share : (n + 1) * share, :] = scratch[pl.ds(start, share), :]


def setup_kernel(pairs, tiles, tile_rows, obs, levels, place, own, left, right, *outs):
    columns, size = obs.shape
    share = size // tiles
    col, tile = place[0, 0], place[0, 1]
    members = place[0, 2].astype(F32)
    lane = lax.broadcasted_iota(jnp.int32, (share, size), 1)
    mine = lane == lax.broadcasted_iota(jnp.int32, (share, size), 0) + tile * share

    def factor(source, which):
        slot, active, batch = standing(col, source, columns)
        level = levels[batch, slot * tiles + which].astype(F32) / 3.0
        return jnp.where(active, level, 0.0)

    for (targets, source), out in zip(pairs, outs):
        for n, target in enumerate(targets):
            slot, _, batch = standing(col, target, columns)
            inside = obs[pl.ds(batch, 1), :] - slot * (tiles * tile_rows)
            row = jnp.zeros((1, size), F32)
            for which in range(tiles):
                hit = (inside >= which * tile_rows) & (inside < (which + 1) * tile_rows)
                row = jnp.where(hit, factor(source, which), row)
            column = jnp.sum(jnp.where(mine, row, 0.0), axis=1, keepdims=True)
            out[n * share : (n + 1) * share, :] = column / members
    for colour in range(NCOL):
        outs[len(pairs) + colour][...] = jnp.full((1, 1), factor(colour, tile)) / members
        slot, active, _ = standing(col, colour, columns)
        value = jnp.where(
            active & (slot == 2), left[...], jnp.where(active & (slot == 0), right[...], own[...])
        )
        pieces = [value[:, n * share : (n + 1) * share] for n in range(tiles)]
        ordered = []
        for step in range(tiles):
            source = lax.rem(tile + tiles - step, tiles)
            piece = pieces[0]
            for n in range(1, tiles):
                piece = jnp.where(source == n, pieces[n], piece)
            ordered.append(piece)
        outs[len(pairs) + NCOL + colour][...] = jnp.concatenate(ordered, axis=1)


def root_kernel(*refs):
    *pieces, variance, out = refs
    observed = jnp.concatenate([piece[...] for piece in pieces], axis=0)
    size, members = observed.shape
    row = lax.broadcasted_iota(jnp.int32, (size, size), 0)
    column = lax.broadcasted_iota(jnp.int32, (size, size), 1)
    eye = jnp.where(row == column, 1.0, 0.0).astype(F32)
    gram = dot_nt(observed, observed) / (members - 1) + eye * variance[...]
    trace = jnp.sum(jnp.sum(gram * eye, axis=1, keepdims=True), axis=0, keepdims=True)
    left = gram / trace
    right_h = halves(1.5 * eye - 0.5 * left)
    left_h = halves(mat_prod(halves(left), right_h))

    def next_term(left_h, right_h):
        return halves(1.5 * eye - 0.5 * mat_prod(right_h, left_h))

    def step(_, pair):
        left_h, right_h = pair
        term_h = next_term(left_h, right_h)
        return halves(mat_prod(left_h, term_h)), halves(mat_prod(term_h, right_h))

    left_h, right_h = lax.fori_loop(1, NS_STEPS - 1, step, (left_h, right_h))
    right = mat_prod(next_term(left_h, right_h), right_h)
    inverse_half = (right / jnp.sqrt(trace)).astype(BF16)
    out[...] = dot(inverse_half, observed).astype(BF16)


def rows_kernel(count, *refs):
    parts, transformed, factor, outs = refs[:count], refs[count], refs[count + 1], refs[count + 2 :]
    rows = parts[0][...]
    for part in parts[1:]:
        rows = rows + part[...]
    source = transformed[...]
    projected = dot_nt(rows.astype(BF16), source).astype(BF16)
    rows = rows - factor[...] * dot(projected, source)
    share = outs[0].shape[0]
    for n, out in enumerate(outs):
        out[...] = rows[n * share : (n + 1) * share].astype(out.dtype)


def sum_kernel(*refs):
    *parts, out = refs
    total = parts[0][...]
    for part in parts[1:]:
        total = total + part[...]
    out[...] = total


def on_device(anomalies, obs_rows, obs_var, taper_level):
    tile_rows, members = anomalies.shape
    batches, size = obs_rows.shape
    columns = lax.axis_size("gx")
    tiles = lax.axis_size("gy")
    share = size // tiles
    col = lax.axis_index("gx")
    tile = lax.axis_index("gy")
    place = jnp.stack([col, tile, jnp.int32(members - 1)]).astype(jnp.int32).reshape(1, 3)
    levels = taper_level.reshape(batches, 3 * tiles)
    everywhere = list(range(columns))

    def kept_of(colour):
        return [c for c in everywhere if (c - colour) % NCOL != 2]

    def hop(value, pairs):
        flat = [
            ((a % columns) * tiles + b % tiles, (c % columns) * tiles + d % tiles)
            for (a, b), (c, d) in pairs
        ]
        return lax.ppermute(value, AXES, flat)

    def along_gy(value, kept, step):
        return hop(value, [((c, n), (c, n + step)) for c in kept for n in range(tiles)])

    def along_gx(value, colour, step):
        trio = (-1, 0, 1)
        pairs = [
            ((b + trio[m], n), (b + trio[(m + step) % 3], n))
            for b in range(colour, columns, NCOL)
            for m in range(3)
            for n in range(tiles)
        ]
        return hop(value, pairs)

    def beside(value, step):
        return hop(value, [((c, n), (c + step, n)) for c in everywhere for n in range(tiles)])

    def pick(colours, dtype, state):
        shape = jax.ShapeDtypeStruct((len(colours) * share, members), dtype)
        return kernel_call(
            functools.partial(pick_kernel, colours),
            [shape] * tiles,
            [state, obs_rows, place],
            "pick",
            2 * size * tile_rows * members * len(colours) * (1 if dtype == BF16 else 3),
            smem=(2,),
            scratch=[pltpu.VMEM((size, members), dtype)],
        )

    def scattered(parts, kept):
        return [parts[0], *[along_gy(parts[n], kept, n) for n in range(1, tiles)]]

    def added(parts):
        return kernel_call(
            sum_kernel,
            jax.ShapeDtypeStruct(parts[0].shape, parts[0].dtype),
            parts,
            "sum",
            1_000_000,
        )

    def collected(rows, colour):
        whole = added([rows, along_gx(rows, colour, 1), along_gx(rows, colour, 2)])
        kept = kept_of(colour)
        return [whole, *[along_gy(whole, kept, step) for step in range(1, tiles)]]

    def transform(pieces, variance):
        return kernel_call(
            root_kernel,
            jax.ShapeDtypeStruct((size, members), BF16),
            [*pieces, variance],
            "root",
            8_000_000_000,
        )

    def move(parts, transformed, factor, dtypes, name="rows"):
        rows = parts[0].shape[0]
        shape = (rows // len(dtypes), members)
        return kernel_call(
            functools.partial(rows_kernel, len(parts)),
            [jax.ShapeDtypeStruct(shape, dtype) for dtype in dtypes],
            [*parts, transformed, factor],
            name,
            4 * rows * size * members,
        )

    together = lax.optimization_barrier
    parts0 = scattered(pick((0,), BF16, anomalies), kept_of(0))
    total0 = added(parts0)
    picked1 = pick((1,), F32, anomalies)
    picked23 = pick((2, 3), F32, anomalies)

    pairs = (((1,), 0), ((2, 3), 0), ((2,), 1), ((3,), 1), ((3,), 2))
    own_var, _ = together((obs_var, total0))
    prepared = kernel_call(
        functools.partial(setup_kernel, pairs, tiles, tile_rows),
        [jax.ShapeDtypeStruct((len(t) * share, 1), F32) for t, _ in pairs]
        + [jax.ShapeDtypeStruct((1, 1), F32)] * NCOL
        + [jax.ShapeDtypeStruct((1, size), F32)] * NCOL,
        [obs_rows, levels, place, obs_var, beside(own_var, 1), beside(own_var, -1)],
        "setup",
        1_000_000,
        smem=(1, 2),
    )
    f10, f230, f21, f31, f32_ = prepared[: len(pairs)]
    tile_factor = prepared[len(pairs) : len(pairs) + NCOL]
    variance = prepared[len(pairs) + NCOL :]

    picked1, total0 = together((picked1, total0))
    parts1 = scattered(picked1, kept_of(1))
    pieces = collected(total0, 0)
    picked23, pieces = together((picked23, pieces))
    parts23 = scattered(picked23, everywhere)
    t0 = transform(pieces, variance[0])

    (next1,) = move(parts1, t0, f10, [BF16])
    (state,) = move([anomalies], t0, tile_factor[0], [F32], "tile")
    pieces = collected(next1, 1)
    var1, state = together((variance[1], state))
    t1 = transform(pieces, var1)

    rows2, rows3 = move(parts23, t0, f230, [F32, F32])
    (next2,) = move([rows2], t1, f21, [BF16])
    (rows3,) = move([rows3], t1, f31, [F32])
    (state,) = move([state], t1, tile_factor[1], [F32], "tile")
    pieces = collected(next2, 2)
    var2, state, rows3 = together((variance[2], state, rows3))
    t2 = transform(pieces, var2)

    (next3,) = move([rows3], t2, f32_, [BF16])
    (state,) = move([state], t2, tile_factor[2], [F32], "tile")
    pieces = collected(next3, 3)
    var3, state = together((variance[3], state))
    t3 = transform(pieces, var3)
    (state,) = move([state], t3, tile_factor[3], [F32], "tile")
    return state


def solution(mesh):
    in_specs = (P(AXES, None), P(), P("gx", None), P())
    return jax.shard_map(
        on_device,
        mesh=mesh,
        in_specs=in_specs,
        out_specs=P(AXES, None),
        check_vma=False,
    )
```

profile of v0, /device:TPU:6, one launch (start us, length us, event | category | flops | bytes accessed | tf_op | source)
XLA Modules:
  0.0 181.5 jit_solution(391981012452606581)
XLA Ops:
  0.1 1.6 copy-done
  1.7 0.8 copy-done.2
  2.5 1.0 pick.3
  3.6 4.3 %collective-permute-start = (bf16[64,1024]{1,0:T(8,128)(2,1)S(1)}, bf16[64,1024]{1,0:T(8,128)(2,1)S(1)}, u32[]{:S(2)}, u32[]{:S(2)}) collective-permute-start(bf16[64,1024]{1,0:T(8,128)(2,1)S(1)} %get-tuple-element.54), channel_id=1, source_target_pairs={{0,1},{1,2},{2,3},{3,0},{4,5},{5,6},{6,7},{7,4},{12,13},{13,14},{1... | collective-permute-start | bytes 393224 | tf_op jit(solution)/shard_map/ppermute | solution.py:207
  7.8 2.6 %collective-permute-start.1 = (bf16[64,1024]{1,0:T(8,128)(2,1)S(1)}, bf16[64,1024]{1,0:T(8,128)(2,1)S(1)}, u32[]{:S(2)}, u32[]{:S(2)}) collective-permute-start(bf16[64,1024]{1,0:T(8,128)(2,1)S(1)} %get-tuple-element.55), channel_id=1, source_target_pairs={{0,2},{1,3},{2,0},{3,1},{4,6},{5,7},{6,4},{7,5},{12,14},{13,15},{1... | collective-permute-start | bytes 393224 | tf_op jit(solution)/shard_map/ppermute | solution.py:207
  10.4 2.1 %collective-permute-start.2 = (bf16[64,1024]{1,0:T(8,128)(2,1)S(1)}, bf16[64,1024]{1,0:T(8,128)(2,1)S(1)}, u32[]{:S(2)}, u32[]{:S(2)}) collective-permute-start(bf16[64,1024]{1,0:T(8,128)(2,1)S(1)} %get-tuple-element.56), channel_id=1, source_target_pairs={{0,3},{1,0},{2,1},{3,2},{4,7},{5,4},{6,5},{7,6},{12,15},{13,12},{1... | collective-permute-start | bytes 393224 | tf_op jit(solution)/shard_map/ppermute | solution.py:207
  12.5 1.8 pick.5
  14.4 2.7 %collective-permute-done.1.refs_2_ = bf16[64,1024]{1,0:T(8,128)(2,1)S(1)} collective-permute-done((bf16[64,1024]{1,0:T(8,128)(2,1)S(1)}, bf16[64,1024]{1,0:T(8,128)(2,1)S(1)}, u32[]{:S(2)}, u32[]{:S(2)}) %collective-permute-start.1) | collective-permute-done | bytes 131104 | tf_op jit(solution)/shard_map/ppermute | solution.py:207
  17.0 2.0 %collective-permute-done.2.refs_3_ = bf16[64,1024]{1,0:T(8,128)(2,1)S(1)} collective-permute-done((bf16[64,1024]{1,0:T(8,128)(2,1)S(1)}, bf16[64,1024]{1,0:T(8,128)(2,1)S(1)}, u32[]{:S(2)}, u32[]{:S(2)}) %collective-permute-start.2) | collective-permute-done | bytes 131104 | tf_op jit(solution)/shard_map/ppermute | solution.py:207
  19.1 7.4 %collective-permute-start.6 = (bf16[64,1024]{1,0:T(8,128)(2,1)S(1)}, bf16[64,1024]{1,0:T(8,128)(2,1)S(1)}, u32[]{:S(2)}, u32[]{:S(2)}) collective-permute-start(bf16[64,1024]{1,0:T(8,128)(2,1)S(1)} %sum.5.refs_0_), channel_id=1, source_target_pairs={{252,4},{253,5},{254,6},{255,7},{0,252},{1,253},{2,254},{3,255},{4... | collective-permute-start | bytes 393224 | tf_op jit(solution)/shard_map/ppermute | solution.py:207
  26.5 1.9 %collective-permute-start.5 = (bf16[64,1024]{1,0:T(8,128)(2,1)S(1)}, bf16[64,1024]{1,0:T(8,128)(2,1)S(1)}, u32[]{:S(2)}, u32[]{:S(2)}) collective-permute-start(bf16[64,1024]{1,0:T(8,128)(2,1)S(1)} %sum.5.refs_0_), channel_id=1, source_target_pairs={{252,0},{253,1},{254,2},{255,3},{0,4},{1,5},{2,6},{3,7},{4,252},{5... | collective-permute-start | bytes 393224 | tf_op jit(solution)/shard_map/ppermute | solution.py:207
  28.4 5.1 %collective-permute-start.4 = (f32[1,256]{1,0:T(1,128)S(1)}, f32[1,256]{1,0:T(1,128)S(1)}, u32[]{:S(2)}, u32[]{:S(2)}) collective-permute-start(f32[1,256]{1,0:T(1,128)S(1)} %copy-done.4), channel_id=1, source_target_pairs={{0,252},{1,253},{2,254},{3,255},{4,0},{5,1},{6,2},{7,3},{8,4},{9,5... | collective-permute-start | bytes 3080 | tf_op jit(solution)/shard_map/ppermute | solution.py:207
  33.6 2.5 %collective-permute-done.5.refs_1_ = bf16[64,1024]{1,0:T(8,128)(2,1)S(1)} collective-permute-done((bf16[64,1024]{1,0:T(8,128)(2,1)S(1)}, bf16[64,1024]{1,0:T(8,128)(2,1)S(1)}, u32[]{:S(2)}, u32[]{:S(2)}) %collective-permute-start.5) | collective-permute-done | bytes 131104 | tf_op jit(solution)/shard_map/ppermute | solution.py:207
  36.2 2.1 %collective-permute-start.9 = (bf16[64,1024]{1,0:T(8,128)(2,1)S(1)}, bf16[64,1024]{1,0:T(8,128)(2,1)}, u32[]{:S(2)}, u32[]{:S(2)}) collective-permute-start(bf16[64,1024]{1,0:T(8,128)(2,1)S(1)} %sum.6.refs_0_), channel_id=1, source_target_pairs={{0,3},{1,0},{2,1},{3,2},{4,7},{5,4},{6,5},{7,6},{12,15},{13,12},{1... | collective-permute-start | bytes 393224 | tf_op jit(solution)/shard_map/ppermute | solution.py:207
  38.2 4.0 %collective-permute-start.8 = (bf16[64,1024]{1,0:T(8,128)(2,1)S(1)}, bf16[64,1024]{1,0:T(8,128)(2,1)}, u32[]{:S(2)}, u32[]{:S(2)}) collective-permute-start(bf16[64,1024]{1,0:T(8,128)(2,1)S(1)} %sum.6.refs_0_), channel_id=1, source_target_pairs={{0,2},{1,3},{2,0},{3,1},{4,6},{5,7},{6,4},{7,5},{12,14},{13,15},{1... | collective-permute-start | bytes 393224 | tf_op jit(solution)/shard_map/ppermute | solution.py:207
  42.2 3.1 %collective-permute-start.7 = (bf16[64,1024]{1,0:T(8,128)(2,1)S(1)}, bf16[64,1024]{1,0:T(8,128)(2,1)}, u32[]{:S(2)}, u32[]{:S(2)}) collective-permute-start(bf16[64,1024]{1,0:T(8,128)(2,1)S(1)} %sum.6.refs_0_), channel_id=1, source_target_pairs={{0,1},{1,2},{2,3},{3,0},{4,5},{5,6},{6,7},{7,4},{12,13},{13,14},{1... | collective-permute-start | bytes 393224 | tf_op jit(solution)/shard_map/ppermute | solution.py:207
  45.3 2.7 %pick.4 = (f32[128,1024]{1,0:T(8,128)S(1)}, f32[128,1024]{1,0:T(8,128)S(1)}, f32[128,1024]{1,0:T(8,128)S(1)}, f32[128,1024]{1,0:T(8,128)S(1)}) custom-call(f32[512,1024]{1,0:T(8,128)S(1)} %copy-done.1, s32[64,256]{1,0:T(8,128)S(1)} %copy-done.2, s32[1,3]{1,0:T(1,128)S(1)} %add_bitcast_fusion.place), custom_call_target="tpu_custom_call" | custom-call | flops 1610612736 | bytes 4259852 | tf_op jit(solution)/shard_map/pick/pallas_call | solution.py:23
  48.0 0.8 copy-done.5
  48.8 0.8 copy-done.7
  49.6 0.8 copy-done.9
  50.4 0.1 copy.6.levels
  50.5 2.8 %collective-permute-start.10 = (f32[64,1024]{1,0:T(8,128)}, f32[64,1024]{1,0:T(8,128)S(1)}, u32[]{:S(2)}, u32[]{:S(2)}) collective-permute-start(f32[64,1024]{1,0:T(8,128)} %copy-done.12), channel_id=1, source_target_pairs={{0,1},{1,2},{2,3},{3,0},{4,5},{5,6},{6,7},{7,4},{8,9},{9,10},{10,1... | collective-permute-start | bytes 786440 | tf_op jit(solution)/shard_map/ppermute | solution.py:207
  53.3 4.0 %collective-permute-start.11 = (f32[64,1024]{1,0:T(8,128)}, f32[64,1024]{1,0:T(8,128)S(1)}, u32[]{:S(2)}, u32[]{:S(2)}) collective-permute-start(f32[64,1024]{1,0:T(8,128)} %copy-done.11), channel_id=1, source_target_pairs={{0,2},{1,3},{2,0},{3,1},{4,6},{5,7},{6,4},{7,5},{8,10},{9,11},{10,... | collective-permute-start | bytes 786440 | tf_op jit(solution)/shard_map/ppermute | solution.py:207
  57.3 1.9 %setup.1 = (f32[64,1]{1,0:T(8,128)S(1)}, f32[128,1]{1,0:T(8,128)S(1)}, f32[64,1]{1,0:T(8,128)S(1)}, f32[64,1]{1,0:T(8,128)S(1)}, f32[64,1]{1,0:T(8,128)S(1)}, /*...) custom-call(s32[64,256]{1,0:T(8,128)S(1)} %copy-done.3, ...), custom_call_target="tpu_custom_call" | custom-call | flops 1000000 | bytes 77340 | tf_op jit(solution)/shard_map/setup/pallas_call | solution.py:23
  59.2 3.3 %collective-permute-start.12 = (f32[64,1024]{1,0:T(8,128)S(1)}, f32[64,1024]{1,0:T(8,128)S(1)}, u32[]{:S(2)}, u32[]{:S(2)}) collective-permute-start(f32[64,1024]{1,0:T(8,128)S(1)} %get-tuple-element.80), channel_id=1, source_target_pairs={{0,3},{1,0},{2,1},{3,2},{4,7},{5,4},{6,5},{7,6},{8,11},{9,8},{10,9... | collective-permute-start | bytes 786440 | tf_op jit(solution)/shard_map/ppermute | solution.py:207
  62.5 9.2 %root.4.refs_1_.refs_4_ = bf16[256,1024]{1,0:T(8,128)(2,1)S(1)} custom-call(bf16[64,1024]{1,0:T(8,128)(2,1)S(1)} %sum.6.refs_0_, bf16[64,1024]{1,0:T(8,128)(2,1)} %collective-permute-done.7.refs_1_, bf16[64,1024]{1,0:T(8,128)(2,1)} %collective-permute-done.8.refs_2_, bf16[64,1024]{1,0:T(8,128)(2,1)} %collective-permute-done.9.refs_3_, ...), custom_call_target="tpu_custom_call" | custom-call | flops 8000000000 | bytes 1049600 | tf_op jit(solution)/shard_map/root/pallas_call | solution.py:23
  71.8 0.6 rows.5.refs_0_
  72.4 1.9 %collective-permute-start.14 = (bf16[64,1024]{1,0:T(8,128)(2,1)S(1)}, bf16[64,1024]{1,0:T(8,128)(2,1)S(1)}, u32[]{:S(2)}, u32[]{:S(2)}) collective-permute-start(bf16[64,1024]{1,0:T(8,128)(2,1)S(1)} %rows.5.refs_0_), channel_id=1, source_target_pairs={{0,8},{1,9},{2,10},{3,11},{4,0},{5,1},{6,2},{7,3},{8,4},{9,5},{10,... | collective-permute-start | bytes 393224 | tf_op jit(solution)/shard_map/ppermute | solution.py:207
  74.3 2.4 %collective-permute-start.13 = (bf16[64,1024]{1,0:T(8,128)(2,1)S(1)}, bf16[64,1024]{1,0:T(8,128)(2,1)S(1)}, u32[]{:S(2)}, u32[]{:S(2)}) collective-permute-start(bf16[64,1024]{1,0:T(8,128)(2,1)S(1)} %rows.5.refs_0_), channel_id=1, source_target_pairs={{0,4},{1,5},{2,6},{3,7},{4,8},{5,9},{6,10},{7,11},{8,0},{9,1},{10,... | collective-permute-start | bytes 393224 | tf_op jit(solution)/shard_map/ppermute | solution.py:207
  76.7 0.1 collective-permute-done.14.refs_2_
  76.8 4.4 %collective-permute-done.13.refs_1_ = bf16[64,1024]{1,0:T(8,128)(2,1)S(1)} collective-permute-done((bf16[64,1024]{1,0:T(8,128)(2,1)S(1)}, bf16[64,1024]{1,0:T(8,128)(2,1)S(1)}, u32[]{:S(2)}, u32[]{:S(2)}) %collective-permute-start.13) | collective-permute-done | bytes 131104 | tf_op jit(solution)/shard_map/ppermute | solution.py:207
  81.2 1.9 %collective-permute-start.17 = (bf16[64,1024]{1,0:T(8,128)(2,1)S(1)}, bf16[64,1024]{1,0:T(8,128)(2,1)S(1)}, u32[]{:S(2)}, u32[]{:S(2)}) collective-permute-start(bf16[64,1024]{1,0:T(8,128)(2,1)S(1)} %sum.7.refs_0_), channel_id=1, source_target_pairs={{0,3},{1,0},{2,1},{3,2},{4,7},{5,4},{6,5},{7,6},{8,11},{9,8},{10,9... | collective-permute-start | bytes 393224 | tf_op jit(solution)/shard_map/ppermute | solution.py:207
  83.1 5.2 %collective-permute-start.16 = (bf16[64,1024]{1,0:T(8,128)(2,1)S(1)}, bf16[64,1024]{1,0:T(8,128)(2,1)S(1)}, u32[]{:S(2)}, u32[]{:S(2)}) collective-permute-start(bf16[64,1024]{1,0:T(8,128)(2,1)S(1)} %sum.7.refs_0_), channel_id=1, source_target_pairs={{0,2},{1,3},{2,0},{3,1},{4,6},{5,7},{6,4},{7,5},{8,10},{9,11},{10,... | collective-permute-start | bytes 393224 | tf_op jit(solution)/shard_map/ppermute | solution.py:207
  88.3 3.1 %collective-permute-start.15 = (bf16[64,1024]{1,0:T(8,128)(2,1)S(1)}, bf16[64,1024]{1,0:T(8,128)(2,1)S(1)}, u32[]{:S(2)}, u32[]{:S(2)}) collective-permute-start(bf16[64,1024]{1,0:T(8,128)(2,1)S(1)} %sum.7.refs_0_), channel_id=1, source_target_pairs={{0,1},{1,2},{2,3},{3,0},{4,5},{5,6},{6,7},{7,4},{8,9},{9,10},{10,1... | collective-permute-start | bytes 393224 | tf_op jit(solution)/shard_map/ppermute | solution.py:207
  91.4 0.1 collective-permute-start.18
  91.5 2.9 %collective-permute-start.19 = (f32[128,1024]{1,0:T(8,128)S(1)}, f32[128,1024]{1,0:T(8,128)S(1)}, u32[]{:S(2)}, u32[]{:S(2)}) collective-permute-start(f32[128,1024]{1,0:T(8,128)S(1)} %copy-done.8), channel_id=1, source_target_pairs={{0,2},{1,3},{2,0},{3,1},{4,6},{5,7},{6,4},{7,5},{8,10},{9,11},{10,... | collective-permute-start | bytes 1572872 | tf_op jit(solution)/shard_map/ppermute | solution.py:207
  94.4 1.9 %tile.4.refs_0_ = f32[512,1024]{1,0:T(8,128)S(1)} custom-call(f32[512,1024]{1,0:T(8,128)S(1)} %copy-done.1, bf16[256,1024]{1,0:T(8,128)(2,1)S(1)} %root.4.refs_1_.refs_4_, f32[1,1]{1,0:T(1,128)} %get-tuple-element.75.refs_2_), custom_call_target="tpu_custom_call" | custom-call | flops 536870912 | bytes 4718596 | tf_op jit(solution)/shard_map/tile/pallas_call | solution.py:23
  96.3 0.5 collective-permute-start.20
  96.8 8.2 %root.5.refs_1_ = bf16[256,1024]{1,0:T(8,128)(2,1)S(1)} custom-call(bf16[64,1024]{1,0:T(8,128)(2,1)S(1)} %sum.7.refs_0_, bf16[64,1024]{1,0:T(8,128)(2,1)S(1)} %collective-permute-done.15.refs_1_, bf16[64,1024]{1,0:T(8,128)(2,1)S(1)} %collective-permute-done.16.refs_2_, bf16[64,1024]{1,0:T(8,128)(2,1)S(1)} %collective-permute-done.17.refs_3_, ...), custom_call_target="tpu_custom_call" | custom-call | flops 8000000000 | bytes 1049600 | tf_op jit(solution)/shard_map/root/pallas_call | solution.py:23
  105.0 2.9 %collective-permute-done.18.refs_1_ = f32[128,1024]{1,0:T(8,128)S(1)} collective-permute-done((f32[128,1024]{1,0:T(8,128)S(1)}, f32[128,1024]{1,0:T(8,128)S(1)}, u32[]{:S(2)}, u32[]{:S(2)}) %collective-permute-start.18) | collective-permute-done | bytes 524320 | tf_op jit(solution)/shard_map/ppermute | solution.py:207
  107.9 0.1 collective-permute-done.19.refs_2_
  108.0 6.8 %collective-permute-done.20.refs_3_ = f32[128,1024]{1,0:T(8,128)S(1)} collective-permute-done((f32[128,1024]{1,0:T(8,128)S(1)}, f32[128,1024]{1,0:T(8,128)S(1)}, u32[]{:S(2)}, u32[]{:S(2)}) %collective-permute-start.20) | collective-permute-done | bytes 524320 | tf_op jit(solution)/shard_map/ppermute | solution.py:207
  114.8 0.6 rows.6
  115.4 0.6 rows.8.refs_0_
  116.0 0.7 collective-permute-start.22
  116.7 0.7 collective-permute-start.21
  117.4 0.7 collective-permute-start.25
  118.1 0.7 collective-permute-start.24
  118.8 0.7 collective-permute-start.23
  119.5 2.0 %tile.5.refs_0_ = f32[512,1024]{1,0:T(8,128)S(1)} custom-call(f32[512,1024]{1,0:T(8,128)S(1)} %tile.4.refs_0_, bf16[256,1024]{1,0:T(8,128)(2,1)S(1)} %root.5.refs_1_, f32[1,1]{1,0:T(1,128)} %get-tuple-element.83.refs_2_), custom_call_target="tpu_custom_call" | custom-call | flops 536870912 | bytes 4718596 | tf_op jit(solution)/shard_map/tile/pallas_call | solution.py:23
  121.4 0.6 rows.7.refs_0_
  122.0 8.2 %root.6.refs_1_ = bf16[256,1024]{1,0:T(8,128)(2,1)S(1)} custom-call(bf16[64,1024]{1,0:T(8,128)(2,1)S(1)} %sum.8.refs_0_, bf16[64,1024]{1,0:T(8,128)(2,1)S(1)} %collective-permute-done.23.refs_1_, bf16[64,1024]{1,0:T(8,128)(2,1)S(1)} %collective-permute-done.24.refs_2_, bf16[64,1024]{1,0:T(8,128)(2,1)S(1)} %collective-permute-done.25.refs_3_, ...), custom_call_target="tpu_custom_call" | custom-call | flops 8000000000 | bytes 1049600 | tf_op jit(solution)/shard_map/root/pallas_call | solution.py:23
  130.2 0.6 rows.9.refs_0_
  130.8 14.1 %collective-permute-start.27 = (bf16[64,1024]{1,0:T(8,128)(2,1)S(1)}, bf16[64,1024]{1,0:T(8,128)(2,1)S(1)}, u32[]{:S(2)}, u32[]{:S(2)}) collective-permute-start(bf16[64,1024]{1,0:T(8,128)(2,1)S(1)} %rows.9.refs_0_), channel_id=1, source_target_pairs={{8,16},{9,17},{10,18},{11,19},{12,8},{13,9},{14,10},{15,11},{16,12... | collective-permute-start | bytes 393224 | tf_op jit(solution)/shard_map/ppermute | solution.py:207
  144.9 5.1 %collective-permute-start.26 = (bf16[64,1024]{1,0:T(8,128)(2,1)S(1)}, bf16[64,1024]{1,0:T(8,128)(2,1)S(1)}, u32[]{:S(2)}, u32[]{:S(2)}) collective-permute-start(bf16[64,1024]{1,0:T(8,128)(2,1)S(1)} %rows.9.refs_0_), channel_id=1, source_target_pairs={{8,12},{9,13},{10,14},{11,15},{12,16},{13,17},{14,18},{15,19},{16,... | collective-permute-start | bytes 393224 | tf_op jit(solution)/shard_map/ppermute | solution.py:207
  150.1 1.0 collective-permute-done.27.refs_2_
  151.1 3.5 %collective-permute-done.26.refs_1_ = bf16[64,1024]{1,0:T(8,128)(2,1)S(1)} collective-permute-done((bf16[64,1024]{1,0:T(8,128)(2,1)S(1)}, bf16[64,1024]{1,0:T(8,128)(2,1)S(1)}, u32[]{:S(2)}, u32[]{:S(2)}) %collective-permute-start.26) | collective-permute-done | bytes 131104 | tf_op jit(solution)/shard_map/ppermute | solution.py:207
  154.6 1.9 %collective-permute-start.30 = (bf16[64,1024]{1,0:T(8,128)(2,1)S(1)}, bf16[64,1024]{1,0:T(8,128)(2,1)S(1)}, u32[]{:S(2)}, u32[]{:S(2)}) collective-permute-start(bf16[64,1024]{1,0:T(8,128)(2,1)S(1)} %sum.9.refs_0_), channel_id=1, source_target_pairs={{0,3},{1,0},{2,1},{3,2},{8,11},{9,8},{10,9},{11,10},{12,15},{13,12... | collective-permute-start | bytes 393224 | tf_op jit(solution)/shard_map/ppermute | solution.py:207
  156.5 6.8 %collective-permute-start.29 = (bf16[64,1024]{1,0:T(8,128)(2,1)S(1)}, bf16[64,1024]{1,0:T(8,128)(2,1)S(1)}, u32[]{:S(2)}, u32[]{:S(2)}) collective-permute-start(bf16[64,1024]{1,0:T(8,128)(2,1)S(1)} %sum.9.refs_0_), channel_id=1, source_target_pairs={{0,2},{1,3},{2,0},{3,1},{8,10},{9,11},{10,8},{11,9},{12,14},{13,15... | collective-permute-start | bytes 393224 | tf_op jit(solution)/shard_map/ppermute | solution.py:207
  163.3 1.9 %collective-permute-start.28 = (bf16[64,1024]{1,0:T(8,128)(2,1)S(1)}, bf16[64,1024]{1,0:T(8,128)(2,1)S(1)}, u32[]{:S(2)}, u32[]{:S(2)}) collective-permute-start(bf16[64,1024]{1,0:T(8,128)(2,1)S(1)} %sum.9.refs_0_), channel_id=1, source_target_pairs={{0,1},{1,2},{2,3},{3,0},{8,9},{9,10},{10,11},{11,8},{12,13},{13,14... | collective-permute-start | bytes 393224 | tf_op jit(solution)/shard_map/ppermute | solution.py:207
  165.2 1.8 %tile.6.refs_0_ = f32[512,1024]{1,0:T(8,128)S(1)} custom-call(f32[512,1024]{1,0:T(8,128)S(1)} %tile.5.refs_0_, bf16[256,1024]{1,0:T(8,128)(2,1)S(1)} %root.6.refs_1_, f32[1,1]{1,0:T(1,128)} %get-tuple-element.95.refs_2_), custom_call_target="tpu_custom_call" | custom-call | flops 536870912 | bytes 4718596 | tf_op jit(solution)/shard_map/tile/pallas_call | solution.py:23
  167.1 3.1 %collective-permute-done.28.refs_1_ = bf16[64,1024]{1,0:T(8,128)(2,1)S(1)} collective-permute-done((bf16[64,1024]{1,0:T(8,128)(2,1)S(1)}, bf16[64,1024]{1,0:T(8,128)(2,1)S(1)}, u32[]{:S(2)}, u32[]{:S(2)}) %collective-permute-start.28) | collective-permute-done | bytes 131104 | tf_op jit(solution)/shard_map/ppermute | solution.py:207
  170.1 8.2 %root.7.refs_1_ = bf16[256,1024]{1,0:T(8,128)(2,1)S(1)} custom-call(bf16[64,1024]{1,0:T(8,128)(2,1)S(1)} %sum.9.refs_0_, bf16[64,1024]{1,0:T(8,128)(2,1)S(1)} %collective-permute-done.28.refs_1_, bf16[64,1024]{1,0:T(8,128)(2,1)S(1)} %collective-permute-done.29.refs_2_, bf16[64,1024]{1,0:T(8,128)(2,1)S(1)} %collective-permute-done.30.refs_3_, ...), custom_call_target="tpu_custom_call" | custom-call | flops 8000000000 | bytes 1049600 | tf_op jit(solution)/shard_map/root/pallas_call | solution.py:23
  178.3 3.2 %tile.7 = f32[512,1024]{1,0:T(8,128)} custom-call(f32[512,1024]{1,0:T(8,128)S(1)} %tile.6.refs_0_, bf16[256,1024]{1,0:T(8,128)(2,1)S(1)} %root.7.refs_1_, f32[1,1]{1,0:T(1,128)} %get-tuple-element.100.refs_2_), custom_call_target="tpu_custom_call" | custom-call | flops 536870912 | bytes 4718596 | tf_op jit(solution)/shard_map/tile/pallas_call | solution.py:23
  (51 shorter events, 0.3 us)
Async XLA Ops:
  0.1 1.6 copy-start
  1.7 0.8 copy-start.2
  3.6 24.9 %copy-start.4 = (f32[1,256]{1,0:T(1,128)S(1)}, f32[1,256]{1,0:T(1,128)}, u32[]{:S(2)}) copy-start(f32[1,256]{1,0:T(1,128)} %own.1) | copy-start | bytes 3076
  3.6 41.8 %copy-start.1 = (f32[512,1024]{1,0:T(8,128)S(1)}, f32[512,1024]{1,0:T(8,128)}, u32[]{:S(2)}) copy-start(f32[512,1024]{1,0:T(8,128)} %refs_0_.1) | copy-start | bytes 6291460
  3.6 10.8 %collective-permute-start = (bf16[64,1024]{1,0:T(8,128)(2,1)S(1)}, bf16[64,1024]{1,0:T(8,128)(2,1)S(1)}, u32[]{:S(2)}, u32[]{:S(2)}) collective-permute-start(bf16[64,1024]{1,0:T(8,128)(2,1)S(1)} %get-tuple-element.54), channel_id=1, source_target_pairs={{0,1},{1,2},{2,3},{3,0},{4,5},{5,6},{6,7},{7,4},{12,13},{13,14},{1... | collective-permute-start | bytes 393224 | tf_op jit(solution)/shard_map/ppermute | solution.py:207
  7.8 9.2 %collective-permute-start.1 = (bf16[64,1024]{1,0:T(8,128)(2,1)S(1)}, bf16[64,1024]{1,0:T(8,128)(2,1)S(1)}, u32[]{:S(2)}, u32[]{:S(2)}) collective-permute-start(bf16[64,1024]{1,0:T(8,128)(2,1)S(1)} %get-tuple-element.55), channel_id=1, source_target_pairs={{0,2},{1,3},{2,0},{3,1},{4,6},{5,7},{6,4},{7,5},{12,14},{13,15},{1... | collective-permute-start | bytes 393224 | tf_op jit(solution)/shard_map/ppermute | solution.py:207
  10.4 8.6 %collective-permute-start.2 = (bf16[64,1024]{1,0:T(8,128)(2,1)S(1)}, bf16[64,1024]{1,0:T(8,128)(2,1)S(1)}, u32[]{:S(2)}, u32[]{:S(2)}) collective-permute-start(bf16[64,1024]{1,0:T(8,128)(2,1)S(1)} %get-tuple-element.56), channel_id=1, source_target_pairs={{0,3},{1,0},{2,1},{3,2},{4,7},{5,4},{6,5},{7,6},{12,15},{13,12},{1... | collective-permute-start | bytes 393224 | tf_op jit(solution)/shard_map/ppermute | solution.py:207
  14.3 27.9 %copy-start.11 = (f32[64,1024]{1,0:T(8,128)}, f32[64,1024]{1,0:T(8,128)S(1)}, u32[]{:S(2)}) copy-start(f32[64,1024]{1,0:T(8,128)S(1)} %get-tuple-element.79) | copy-start | bytes 786436
  14.3 31.0 %copy-start.12 = (f32[64,1024]{1,0:T(8,128)}, f32[64,1024]{1,0:T(8,128)S(1)}, u32[]{:S(2)}) copy-start(f32[64,1024]{1,0:T(8,128)S(1)} %get-tuple-element.78) | copy-start | bytes 786436
  19.1 14.5 %collective-permute-start.6 = (bf16[64,1024]{1,0:T(8,128)(2,1)S(1)}, bf16[64,1024]{1,0:T(8,128)(2,1)S(1)}, u32[]{:S(2)}, u32[]{:S(2)}) collective-permute-start(bf16[64,1024]{1,0:T(8,128)(2,1)S(1)} %sum.5.refs_0_), channel_id=1, source_target_pairs={{252,4},{253,5},{254,6},{255,7},{0,252},{1,253},{2,254},{3,255},{4... | collective-permute-start | bytes 393224 | tf_op jit(solution)/shard_map/ppermute | solution.py:207
  26.5 9.6 %collective-permute-start.5 = (bf16[64,1024]{1,0:T(8,128)(2,1)S(1)}, bf16[64,1024]{1,0:T(8,128)(2,1)S(1)}, u32[]{:S(2)}, u32[]{:S(2)}) collective-permute-start(bf16[64,1024]{1,0:T(8,128)(2,1)S(1)} %sum.5.refs_0_), channel_id=1, source_target_pairs={{252,0},{253,1},{254,2},{255,3},{0,4},{1,5},{2,6},{3,7},{4,252},{5... | collective-permute-start | bytes 393224 | tf_op jit(solution)/shard_map/ppermute | solution.py:207
  28.4 22.1 %collective-permute-start.4 = (f32[1,256]{1,0:T(1,128)S(1)}, f32[1,256]{1,0:T(1,128)S(1)}, u32[]{:S(2)}, u32[]{:S(2)}) collective-permute-start(f32[1,256]{1,0:T(1,128)S(1)} %copy-done.4), channel_id=1, source_target_pairs={{0,252},{1,253},{2,254},{3,255},{4,0},{5,1},{6,2},{7,3},{8,4},{9,5... | collective-permute-start | bytes 3080 | tf_op jit(solution)/shard_map/ppermute | solution.py:207
  33.6 19.7 %collective-permute-start.3 = (f32[1,256]{1,0:T(1,128)S(1)}, f32[1,256]{1,0:T(1,128)S(1)}, u32[]{:S(2)}, u32[]{:S(2)}) collective-permute-start(f32[1,256]{1,0:T(1,128)S(1)} %copy-done.4), channel_id=1, source_target_pairs={{0,4},{1,5},{2,6},{3,7},{4,8},{5,9},{6,10},{7,11},{8,12},{9,13},{1... | collective-permute-start | bytes 3080 | tf_op jit(solution)/shard_map/ppermute | solution.py:207
  36.1 14.3 %copy-start.13 = (s32[64,3,4]{0,2,1:T(4,128)S(1)}, s32[64,3,4]{0,2,1:T(4,128)}, u32[]{:S(2)}) copy-start(s32[64,3,4]{0,2,1:T(4,128)} %param.7) | copy-start | bytes 9220
  36.2 21.1 %copy-start.3 = (s32[64,256]{1,0:T(8,128)S(1)}, s32[64,256]{1,0:T(8,128)}, u32[]{:S(2)}) copy-start(s32[64,256]{1,0:T(8,128)} %obs.7) | copy-start | bytes 196612
  36.2 23.0 %collective-permute-start.9 = (bf16[64,1024]{1,0:T(8,128)(2,1)S(1)}, bf16[64,1024]{1,0:T(8,128)(2,1)}, u32[]{:S(2)}, u32[]{:S(2)}) collective-permute-start(bf16[64,1024]{1,0:T(8,128)(2,1)S(1)} %sum.6.refs_0_), channel_id=1, source_target_pairs={{0,3},{1,0},{2,1},{3,2},{4,7},{5,4},{6,5},{7,6},{12,15},{13,12},{1... | collective-permute-start | bytes 393224 | tf_op jit(solution)/shard_map/ppermute | solution.py:207
  38.2 24.3 %collective-permute-start.8 = (bf16[64,1024]{1,0:T(8,128)(2,1)S(1)}, bf16[64,1024]{1,0:T(8,128)(2,1)}, u32[]{:S(2)}, u32[]{:S(2)}) collective-permute-start(bf16[64,1024]{1,0:T(8,128)(2,1)S(1)} %sum.6.refs_0_), channel_id=1, source_target_pairs={{0,2},{1,3},{2,0},{3,1},{4,6},{5,7},{6,4},{7,5},{12,14},{13,15},{1... | collective-permute-start | bytes 393224 | tf_op jit(solution)/shard_map/ppermute | solution.py:207
  42.2 20.3 %collective-permute-start.7 = (bf16[64,1024]{1,0:T(8,128)(2,1)S(1)}, bf16[64,1024]{1,0:T(8,128)(2,1)}, u32[]{:S(2)}, u32[]{:S(2)}) collective-permute-start(bf16[64,1024]{1,0:T(8,128)(2,1)S(1)} %sum.6.refs_0_), channel_id=1, source_target_pairs={{0,1},{1,2},{2,3},{3,0},{4,5},{5,6},{6,7},{7,4},{12,13},{13,14},{1... | collective-permute-start | bytes 393224 | tf_op jit(solution)/shard_map/ppermute | solution.py:207
  48.0 0.8 copy-start.5
  48.8 0.8 copy-start.7
  49.6 0.8 copy-start.9
  50.5 21.2 %collective-permute-start.10 = (f32[64,1024]{1,0:T(8,128)}, f32[64,1024]{1,0:T(8,128)S(1)}, u32[]{:S(2)}, u32[]{:S(2)}) collective-permute-start(f32[64,1024]{1,0:T(8,128)} %copy-done.12), channel_id=1, source_target_pairs={{0,1},{1,2},{2,3},{3,0},{4,5},{5,6},{6,7},{7,4},{8,9},{9,10},{10,1... | collective-permute-start | bytes 786440 | tf_op jit(solution)/shard_map/ppermute | solution.py:207
  53.3 18.5 %collective-permute-start.11 = (f32[64,1024]{1,0:T(8,128)}, f32[64,1024]{1,0:T(8,128)S(1)}, u32[]{:S(2)}, u32[]{:S(2)}) collective-permute-start(f32[64,1024]{1,0:T(8,128)} %copy-done.11), channel_id=1, source_target_pairs={{0,2},{1,3},{2,0},{3,1},{4,6},{5,7},{6,4},{7,5},{8,10},{9,11},{10,... | collective-permute-start | bytes 786440 | tf_op jit(solution)/shard_map/ppermute | solution.py:207
  59.2 12.6 %collective-permute-start.12 = (f32[64,1024]{1,0:T(8,128)S(1)}, f32[64,1024]{1,0:T(8,128)S(1)}, u32[]{:S(2)}, u32[]{:S(2)}) collective-permute-start(f32[64,1024]{1,0:T(8,128)S(1)} %get-tuple-element.80), channel_id=1, source_target_pairs={{0,3},{1,0},{2,1},{3,2},{4,7},{5,4},{6,5},{7,6},{8,11},{9,8},{10,9... | collective-permute-start | bytes 786440 | tf_op jit(solution)/shard_map/ppermute | solution.py:207
  71.7 19.7 %copy-start.10 = (f32[128,1024]{1,0:T(8,128)S(1)}, f32[128,1024]{1,0:T(8,128)}, u32[]{:S(2)}) copy-start(f32[128,1024]{1,0:T(8,128)} %copy-done.9) | copy-start | bytes 1572868
  71.8 19.8 %copy-start.8 = (f32[128,1024]{1,0:T(8,128)S(1)}, f32[128,1024]{1,0:T(8,128)}, u32[]{:S(2)}) copy-start(f32[128,1024]{1,0:T(8,128)} %copy-done.7) | copy-start | bytes 1572868
  72.4 4.4 %collective-permute-start.14 = (bf16[64,1024]{1,0:T(8,128)(2,1)S(1)}, bf16[64,1024]{1,0:T(8,128)(2,1)S(1)}, u32[]{:S(2)}, u32[]{:S(2)}) collective-permute-start(bf16[64,1024]{1,0:T(8,128)(2,1)S(1)} %rows.5.refs_0_), channel_id=1, source_target_pairs={{0,8},{1,9},{2,10},{3,11},{4,0},{5,1},{6,2},{7,3},{8,4},{9,5},{10,... | collective-permute-start | bytes 393224 | tf_op jit(solution)/shard_map/ppermute | solution.py:207
  74.3 6.9 %collective-permute-start.13 = (bf16[64,1024]{1,0:T(8,128)(2,1)S(1)}, bf16[64,1024]{1,0:T(8,128)(2,1)S(1)}, u32[]{:S(2)}, u32[]{:S(2)}) collective-permute-start(bf16[64,1024]{1,0:T(8,128)(2,1)S(1)} %rows.5.refs_0_), channel_id=1, source_target_pairs={{0,4},{1,5},{2,6},{3,7},{4,8},{5,9},{6,10},{7,11},{8,0},{9,1},{10,... | collective-permute-start | bytes 393224 | tf_op jit(solution)/shard_map/ppermute | solution.py:207
  81.2 15.1 %collective-permute-start.17 = (bf16[64,1024]{1,0:T(8,128)(2,1)S(1)}, bf16[64,1024]{1,0:T(8,128)(2,1)S(1)}, u32[]{:S(2)}, u32[]{:S(2)}) collective-permute-start(bf16[64,1024]{1,0:T(8,128)(2,1)S(1)} %sum.7.refs_0_), channel_id=1, source_target_pairs={{0,3},{1,0},{2,1},{3,2},{4,7},{5,4},{6,5},{7,6},{8,11},{9,8},{10,9... | collective-permute-start | bytes 393224 | tf_op jit(solution)/shard_map/ppermute | solution.py:207
  83.1 13.7 %collective-permute-start.16 = (bf16[64,1024]{1,0:T(8,128)(2,1)S(1)}, bf16[64,1024]{1,0:T(8,128)(2,1)S(1)}, u32[]{:S(2)}, u32[]{:S(2)}) collective-permute-start(bf16[64,1024]{1,0:T(8,128)(2,1)S(1)} %sum.7.refs_0_), channel_id=1, source_target_pairs={{0,2},{1,3},{2,0},{3,1},{4,6},{5,7},{6,4},{7,5},{8,10},{9,11},{10,... | collective-permute-start | bytes 393224 | tf_op jit(solution)/shard_map/ppermute | solution.py:207
  88.3 8.5 %collective-permute-start.15 = (bf16[64,1024]{1,0:T(8,128)(2,1)S(1)}, bf16[64,1024]{1,0:T(8,128)(2,1)S(1)}, u32[]{:S(2)}, u32[]{:S(2)}) collective-permute-start(bf16[64,1024]{1,0:T(8,128)(2,1)S(1)} %sum.7.refs_0_), channel_id=1, source_target_pairs={{0,1},{1,2},{2,3},{3,0},{4,5},{5,6},{6,7},{7,4},{8,9},{9,10},{10,1... | collective-permute-start | bytes 393224 | tf_op jit(solution)/shard_map/ppermute | solution.py:207
  91.4 16.5 %collective-permute-start.18 = (f32[128,1024]{1,0:T(8,128)S(1)}, f32[128,1024]{1,0:T(8,128)S(1)}, u32[]{:S(2)}, u32[]{:S(2)}) collective-permute-start(f32[128,1024]{1,0:T(8,128)S(1)} %copy-done.10), channel_id=1, source_target_pairs={{0,1},{1,2},{2,3},{3,0},{4,5},{5,6},{6,7},{7,4},{8,9},{9,10},{10,1... | collective-permute-start | bytes 1572872 | tf_op jit(solution)/shard_map/ppermute | solution.py:207
  91.5 16.5 %collective-permute-start.19 = (f32[128,1024]{1,0:T(8,128)S(1)}, f32[128,1024]{1,0:T(8,128)S(1)}, u32[]{:S(2)}, u32[]{:S(2)}) collective-permute-start(f32[128,1024]{1,0:T(8,128)S(1)} %copy-done.8), channel_id=1, source_target_pairs={{0,2},{1,3},{2,0},{3,1},{4,6},{5,7},{6,4},{7,5},{8,10},{9,11},{10,... | collective-permute-start | bytes 1572872 | tf_op jit(solution)/shard_map/ppermute | solution.py:207
  94.4 1.9 %copy-start.6 = (f32[128,1024]{1,0:T(8,128)S(1)}, f32[128,1024]{1,0:T(8,128)}, u32[]{:S(2)}) copy-start(f32[128,1024]{1,0:T(8,128)} %copy-done.5) | copy-start | bytes 1572868
  96.3 18.5 %collective-permute-start.20 = (f32[128,1024]{1,0:T(8,128)S(1)}, f32[128,1024]{1,0:T(8,128)S(1)}, u32[]{:S(2)}, u32[]{:S(2)}) collective-permute-start(f32[128,1024]{1,0:T(8,128)S(1)} %copy-done.6), channel_id=1, source_target_pairs={{0,3},{1,0},{2,1},{3,2},{4,7},{5,4},{6,5},{7,6},{8,11},{9,8},{10,9... | collective-permute-start | bytes 1572872 | tf_op jit(solution)/shard_map/ppermute | solution.py:207
  116.0 1.4 collective-permute-start.22
  116.7 0.7 collective-permute-start.21
  117.4 4.6 %collective-permute-start.25 = (bf16[64,1024]{1,0:T(8,128)(2,1)S(1)}, bf16[64,1024]{1,0:T(8,128)(2,1)S(1)}, u32[]{:S(2)}, u32[]{:S(2)}) collective-permute-start(bf16[64,1024]{1,0:T(8,128)(2,1)S(1)} %sum.8.refs_0_), channel_id=1, source_target_pairs={{4,7},{5,4},{6,5},{7,6},{8,11},{9,8},{10,9},{11,10},{12,15},{13,12... | collective-permute-start | bytes 393224 | tf_op jit(solution)/shard_map/ppermute | solution.py:207
  118.1 3.9 %collective-permute-start.24 = (bf16[64,1024]{1,0:T(8,128)(2,1)S(1)}, bf16[64,1024]{1,0:T(8,128)(2,1)S(1)}, u32[]{:S(2)}, u32[]{:S(2)}) collective-permute-start(bf16[64,1024]{1,0:T(8,128)(2,1)S(1)} %sum.8.refs_0_), channel_id=1, source_target_pairs={{4,6},{5,7},{6,4},{7,5},{8,10},{9,11},{10,8},{11,9},{12,14},{13,15... | collective-permute-start | bytes 393224 | tf_op jit(solution)/shard_map/ppermute | solution.py:207
  118.8 3.2 %collective-permute-start.23 = (bf16[64,1024]{1,0:T(8,128)(2,1)S(1)}, bf16[64,1024]{1,0:T(8,128)(2,1)S(1)}, u32[]{:S(2)}, u32[]{:S(2)}) collective-permute-start(bf16[64,1024]{1,0:T(8,128)(2,1)S(1)} %sum.8.refs_0_), channel_id=1, source_target_pairs={{4,5},{5,6},{6,7},{7,4},{8,9},{9,10},{10,11},{11,8},{12,13},{13,14... | collective-permute-start | bytes 393224 | tf_op jit(solution)/shard_map/ppermute | solution.py:207
  130.8 20.3 %collective-permute-start.27 = (bf16[64,1024]{1,0:T(8,128)(2,1)S(1)}, bf16[64,1024]{1,0:T(8,128)(2,1)S(1)}, u32[]{:S(2)}, u32[]{:S(2)}) collective-permute-start(bf16[64,1024]{1,0:T(8,128)(2,1)S(1)} %rows.9.refs_0_), channel_id=1, source_target_pairs={{8,16},{9,17},{10,18},{11,19},{12,8},{13,9},{14,10},{15,11},{16,12... | collective-permute-start | bytes 393224 | tf_op jit(solution)/shard_map/ppermute | solution.py:207
  144.9 9.6 %collective-permute-start.26 = (bf16[64,1024]{1,0:T(8,128)(2,1)S(1)}, bf16[64,1024]{1,0:T(8,128)(2,1)S(1)}, u32[]{:S(2)}, u32[]{:S(2)}) collective-permute-start(bf16[64,1024]{1,0:T(8,128)(2,1)S(1)} %rows.9.refs_0_), channel_id=1, source_target_pairs={{8,12},{9,13},{10,14},{11,15},{12,16},{13,17},{14,18},{15,19},{16,... | collective-permute-start | bytes 393224 | tf_op jit(solution)/shard_map/ppermute | solution.py:207
  154.6 12.5 %collective-permute-start.30 = (bf16[64,1024]{1,0:T(8,128)(2,1)S(1)}, bf16[64,1024]{1,0:T(8,128)(2,1)S(1)}, u32[]{:S(2)}, u32[]{:S(2)}) collective-permute-start(bf16[64,1024]{1,0:T(8,128)(2,1)S(1)} %sum.9.refs_0_), channel_id=1, source_target_pairs={{0,3},{1,0},{2,1},{3,2},{8,11},{9,8},{10,9},{11,10},{12,15},{13,12... | collective-permute-start | bytes 393224 | tf_op jit(solution)/shard_map/ppermute | solution.py:207
  156.5 10.5 %collective-permute-start.29 = (bf16[64,1024]{1,0:T(8,128)(2,1)S(1)}, bf16[64,1024]{1,0:T(8,128)(2,1)S(1)}, u32[]{:S(2)}, u32[]{:S(2)}) collective-permute-start(bf16[64,1024]{1,0:T(8,128)(2,1)S(1)} %sum.9.refs_0_), channel_id=1, source_target_pairs={{0,2},{1,3},{2,0},{3,1},{8,10},{9,11},{10,8},{11,9},{12,14},{13,15... | collective-permute-start | bytes 393224 | tf_op jit(solution)/shard_map/ppermute | solution.py:207
  163.3 6.9 %collective-permute-start.28 = (bf16[64,1024]{1,0:T(8,128)(2,1)S(1)}, bf16[64,1024]{1,0:T(8,128)(2,1)S(1)}, u32[]{:S(2)}, u32[]{:S(2)}) collective-permute-start(bf16[64,1024]{1,0:T(8,128)(2,1)S(1)} %sum.9.refs_0_), channel_id=1, source_target_pairs={{0,1},{1,2},{2,3},{3,0},{8,9},{9,10},{10,11},{11,8},{12,13},{13,14... | collective-permute-start | bytes 393224 | tf_op jit(solution)/shard_map/ppermute | solution.py:207
where the time goes:
time: 184 us; the launch traced here: 182 us
  starting transfers between devices  93.7 us (51%)
  Pallas kernels  53 us (29%)
  waiting for transfers between devices  29.1 us (16%)
  local copies, waits for them, and re-layouts  4.99 us (3%)
    ppermute x31, starting transfers between devices, hop(): return lax.ppermute(value, AXES, flat)  93.7 us
    pallas_call x22, Pallas kernels, kernel_call(): pl.pallas_call(body, out_shape=out, in_specs=[scalar if n in smem else wh...  53 us
    ppermute x31, waiting for transfers between devices, hop(): return lax.ppermute(value, AXES, flat)  29.1 us
    unnamed x28, local copies, waits for them, and re-layouts  4.89 us
  transfers between devices with their start and end apart: 31, of which 11 were waited for; matrix products, arithmetic and copies ran while one was open for 0% of the time, Pallas kernels for 17%

commit v1 on v0

v1 whole, which is shorter than its diff:
```python
import functools

import jax
import jax.numpy as jnp
from jax import lax
from jax.experimental import pallas as pl
from jax.experimental.pallas import tpu as pltpu
from jax.sharding import PartitionSpec as P

NCOL = 4
NS_STEPS = 12
AXES = ("gx", "gy")
VMEM_LIMIT = 20 << 20
INTERPRET = False
F32 = jnp.float32
BF16 = jnp.bfloat16


def kernel_call(body, out, args, name, flops, smem=()):
    whole = pl.BlockSpec(memory_space=pltpu.VMEM)
    scalar = pl.BlockSpec(memory_space=pltpu.SMEM)
    leaves = [*args, *jax.tree.leaves(out)]
    return pl.pallas_call(
        body,
        out_shape=out,
        in_specs=[scalar if n in smem else whole for n in range(len(args))],
        out_specs=jax.tree.map(lambda _: whole, out),
        name=name,
        interpret=INTERPRET,
        cost_estimate=pl.CostEstimate(
            flops=flops,
            bytes_accessed=sum(leaf.size * leaf.dtype.itemsize for leaf in leaves),
            transcendentals=0,
        ),
        compiler_params=pltpu.CompilerParams(vmem_limit_bytes=VMEM_LIMIT),
    )(*args)


def dot(left, right):
    return jnp.dot(left, right, preferred_element_type=F32)


def dot_nt(left, right):
    return lax.dot_general(
        left, right, (((1,), (1,)), ((), ())), preferred_element_type=F32
    )


def dot_tn(left, right):
    return lax.dot_general(
        left, right, (((0,), (0,)), ((), ())), preferred_element_type=F32
    )


def halves(value):
    high = value.astype(BF16)
    return high, (value - high.astype(F32)).astype(BF16)


def mat_prod(left, right):
    return dot(left[0], right[0]) + (dot(left[0], right[1]) + dot(left[1], right[0]))


def standing(col, colour, columns):
    offset = lax.rem(col + (NCOL - colour), NCOL)
    slot = jnp.where(offset == 1, 2, jnp.where(offset == 3, 0, 1))
    return slot, offset != 2, lax.rem(col - slot + 1 + columns, columns)


def pick_kernel(tiles, colours, state, obs, place, out):
    tile_rows = state.shape[0]
    columns, size = obs.shape
    share = size // tiles
    col, tile = place[0, 0], place[0, 1]
    rest = state[...]
    parts = [rest.astype(BF16)]
    if out.dtype == F32:
        rest = rest - parts[0].astype(F32)
        parts.append(rest.astype(BF16))
        parts.append((rest - parts[1].astype(F32)).astype(BF16))
    for n, colour in enumerate(colours):
        slot, active, batch = standing(col, colour, columns)
        first = jnp.where(active, (slot * tiles + tile) * tile_rows, -(1 << 20))
        local = obs[pl.ds(batch, 1), :] - first
        spots = lax.broadcasted_iota(jnp.int32, (tile_rows, size), 0)
        chosen = jnp.where(spots == local, 1.0, 0.0).astype(BF16)
        picked = dot_tn(chosen, parts[0])
        for part in parts[1:]:
            picked = picked + dot_tn(chosen, part)
        picked = picked.astype(out.dtype)
        for m in range(tiles):
            start = (m * len(colours) + n) * share
            out[start : start + share, :] = picked[m * share : (m + 1) * share]


def setup_kernel(pairs, tiles, tile_rows, obs, levels, place, own, left, right, *outs):
    columns, size = obs.shape
    share = size // tiles
    col, tile = place[0, 0], place[0, 1]
    members = place[0, 2].astype(F32)
    lane = lax.broadcasted_iota(jnp.int32, (share, size), 1)
    mine = lane == lax.broadcasted_iota(jnp.int32, (share, size), 0) + tile * share

    def factor(source, which):
        slot, active, batch = standing(col, source, columns)
        level = levels[batch, slot * tiles + which].astype(F32) / 3.0
        return jnp.where(active, level, 0.0)

    for (targets, source), out in zip(pairs, outs):
        for n, target in enumerate(targets):
            slot, _, batch = standing(col, target, columns)
            inside = obs[pl.ds(batch, 1), :] - slot * (tiles * tile_rows)
            row = jnp.zeros((1, size), F32)
            for which in range(tiles):
                hit = (inside >= which * tile_rows) & (inside < (which + 1) * tile_rows)
                row = jnp.where(hit, factor(source, which), row)
            column = jnp.sum(jnp.where(mine, row, 0.0), axis=1, keepdims=True)
            out[n * share : (n + 1) * share, :] = column / members
    for colour in range(NCOL):
        outs[len(pairs) + colour][...] = jnp.full((1, 1), factor(colour, tile)) / members
        slot, active, _ = standing(col, colour, columns)
        value = jnp.where(
            active & (slot == 2), left[...], jnp.where(active & (slot == 0), right[...], own[...])
        )
        outs[len(pairs) + NCOL + colour][...] = value


def root_kernel(pieces, variance, out):
    observed = pieces[...]
    size, members = observed.shape
    row = lax.broadcasted_iota(jnp.int32, (size, size), 0)
    column = lax.broadcasted_iota(jnp.int32, (size, size), 1)
    eye = jnp.where(row == column, 1.0, 0.0).astype(F32)
    gram = dot_nt(observed, observed) / (members - 1) + eye * variance[...]
    trace = jnp.sum(jnp.sum(gram * eye, axis=1, keepdims=True), axis=0, keepdims=True)
    left = gram / trace
    right_h = halves(1.5 * eye - 0.5 * left)
    left_h = halves(mat_prod(halves(left), right_h))

    def next_term(left_h, right_h):
        return halves(1.5 * eye - 0.5 * mat_prod(right_h, left_h))

    def step(_, pair):
        left_h, right_h = pair
        term_h = next_term(left_h, right_h)
        return halves(mat_prod(left_h, term_h)), halves(mat_prod(term_h, right_h))

    left_h, right_h = lax.fori_loop(1, NS_STEPS - 1, step, (left_h, right_h))
    right = mat_prod(next_term(left_h, right_h), right_h)
    inverse_half = (right / jnp.sqrt(trace)).astype(BF16)
    out[...] = dot(inverse_half, observed).astype(BF16)


def summed(parts, count):
    rows = parts.shape[0] // count
    total = parts[:rows, :]
    for n in range(1, count):
        total = total + parts[n * rows : (n + 1) * rows, :]
    return total


def rows_kernel(count, parts, *refs):
    *pairs, out = refs
    rows = summed(parts, count)
    for transformed, factor in zip(pairs[::2], pairs[1::2]):
        source = transformed[...]
        projected = dot_nt(rows.astype(BF16), source).astype(BF16)
        rows = rows - factor[...] * dot(projected, source)
    out[...] = rows.astype(out.dtype)


def sum_kernel(count, parts, out):
    out[...] = summed(parts, count)


def copies_kernel(own, first, second, out):
    total = (own[...] + first[...]) + second[...]
    rows = total.shape[0]
    for n in range(out.shape[0] // rows):
        out[n * rows : (n + 1) * rows, :] = total


def on_device(anomalies, obs_rows, obs_var, taper_level):
    tile_rows, members = anomalies.shape
    batches, size = obs_rows.shape
    columns = lax.axis_size("gx")
    tiles = lax.axis_size("gy")
    share = size // tiles
    col = lax.axis_index("gx")
    tile = lax.axis_index("gy")
    place = jnp.stack([col, tile, jnp.int32(members - 1)]).astype(jnp.int32).reshape(1, 3)
    levels = taper_level.reshape(batches, 3 * tiles)
    everywhere = list(range(columns))

    def hop(value, pairs):
        flat = [
            ((a % columns) * tiles + b % tiles, (c % columns) * tiles + d % tiles)
            for (a, b), (c, d) in pairs
        ]
        return lax.ppermute(value, AXES, flat)

    def over_gy(value):
        rows = value.shape[0]
        parts = value.reshape(tiles, rows // tiles, members)
        return lax.all_to_all(parts, "gy", 0, 0, tiled=True).reshape(rows, members)

    def along_gx(value, colour, step):
        trio = (-1, 0, 1)
        pairs = [
            ((b + trio[m], n), (b + trio[(m + step) % 3], n))
            for b in range(colour, columns, NCOL)
            for m in range(3)
            for n in range(tiles)
        ]
        return hop(value, pairs)

    def beside(value, step):
        return hop(value, [((c, n), (c + step, n)) for c in everywhere for n in range(tiles)])

    def pick(colours, dtype, state):
        return kernel_call(
            functools.partial(pick_kernel, tiles, colours),
            jax.ShapeDtypeStruct((len(colours) * size, members), dtype),
            [state, obs_rows, place],
            "pick",
            2 * size * tile_rows * members * len(colours) * (1 if dtype == BF16 else 3),
            smem=(2,),
        )

    def collected(rows, colour):
        args = [rows, along_gx(rows, colour, 1), along_gx(rows, colour, 2)]
        shape = jax.ShapeDtypeStruct((size, members), BF16)
        return over_gy(kernel_call(copies_kernel, shape, args, "copies", 1_000_000))

    def transform(pieces, variance):
        return kernel_call(
            root_kernel,
            jax.ShapeDtypeStruct((size, members), BF16),
            [pieces, variance],
            "root",
            8_000_000_000,
        )

    def move(parts, count, sources, dtype, name="rows"):
        rows = parts.shape[0] // count
        return kernel_call(
            functools.partial(rows_kernel, count),
            jax.ShapeDtypeStruct((rows, members), dtype),
            [parts, *[ref for pair in sources for ref in pair]],
            name,
            4 * rows * size * members * len(sources),
        )

    together = lax.optimization_barrier
    parts0 = over_gy(pick((0,), BF16, anomalies))
    total0 = kernel_call(
        functools.partial(sum_kernel, tiles),
        jax.ShapeDtypeStruct((share, members), BF16),
        [parts0],
        "sum",
        1_000_000,
    )
    picked = [None, *[pick((colour,), F32, anomalies) for colour in range(1, NCOL)]]

    pairs = [((target,), source) for target in range(1, NCOL) for source in range(target)]
    own_var, _ = together((obs_var, total0))
    prepared = kernel_call(
        functools.partial(setup_kernel, pairs, tiles, tile_rows),
        [jax.ShapeDtypeStruct((len(t) * share, 1), F32) for t, _ in pairs]
        + [jax.ShapeDtypeStruct((1, 1), F32)] * NCOL
        + [jax.ShapeDtypeStruct((1, size), F32)] * NCOL,
        [obs_rows, levels, place, obs_var, beside(own_var, 1), beside(own_var, -1)],
        "setup",
        1_000_000,
        smem=(1, 2),
    )
    row_factor = {(t[0], source): out for (t, source), out in zip(pairs, prepared)}
    tile_factor = prepared[len(pairs) : len(pairs) + NCOL]
    variance = prepared[len(pairs) + NCOL :]

    state = anomalies
    rows = total0
    done = []
    for colour in range(NCOL):
        pieces = collected(rows, colour)
        if colour < NCOL - 1:
            coming, pieces = together((picked[colour + 1], pieces))
            parts = over_gy(coming)
        var, state = together((variance[colour], state))
        done.append(transform(pieces, var))
        state_factor = [(done[colour], tile_factor[colour])]
        if colour < NCOL - 1:
            sources = [(done[n], row_factor[colour + 1, n]) for n in range(colour + 1)]
            rows = move(parts, tiles, sources, BF16)
        state = move(state, 1, state_factor, F32, "tile")
    return state


def solution(mesh):
    in_specs = (P(AXES, None), P(), P("gx", None), P())
    return jax.shard_map(
        on_device,
        mesh=mesh,
        in_specs=in_specs,
        out_specs=P(AXES, None),
        check_vma=False,
    )
```

time: 184 us -> 188 us (1.022)
  the two profiles are of different devices: /device:TPU:6 before, /device:TPU:8 now
where the time goes in v1:
time: 188 us; the launch traced here: 187 us
  Pallas kernels  60.9 us (32%)
  starting transfers between devices  59.3 us (32%)
  waiting for transfers between devices  40.7 us (22%)
  blocking collectives  13.7 us (7%)
  local copies, waits for them, and re-layouts  12.2 us (6%)
    pallas_call x21, Pallas kernels, kernel_call(): pl.pallas_call(body, out_shape=out, in_specs=[scalar if n in smem else wh...  60.9 us
    all_to_all x7, starting transfers between devices, over_gy(): return lax.all_to_all(parts, 'gy', 0, 0, tiled=True).reshape(rows, members)  30.3 us
    ppermute x10, starting transfers between devices, hop(): return lax.ppermute(value, AXES, flat)  29.1 us
    all_to_all x7, waiting for transfers between devices, over_gy(): return lax.all_to_all(parts, 'gy', 0, 0, tiled=True).reshape(rows, members)  21.2 us
    ppermute x10, waiting for transfers between devices, hop(): return lax.ppermute(value, AXES, flat)  19.5 us
    all_to_all x1, blocking collectives, over_gy(): return lax.all_to_all(parts, 'gy', 0, 0, tiled=True).reshape(rows, members)  13.7 us
    unnamed x40, local copies, waits for them, and re-layouts  12.1 us
  transfers between devices with their start and end apart: 17, of which 12 were waited for; matrix products, arithmetic and copies ran while one was open for 0% of the time, Pallas kernels for 21%

profile of v1, /device:TPU:8, one launch (start us, length us, event | category | flops | bytes accessed | tf_op | source)
XLA Modules:
  0.0 187.2 jit_solution(13956647709367707220)
XLA Ops:
  0.0 0.1 add_bitcast_fusion.place
  0.1 1.6 copy-done
  1.7 0.8 copy-done.14
  2.5 1.0 pick.4
  3.5 0.0 copy-start.15
  3.6 13.7 %all_to_all.40 = bf16[4,64,1024]{2,1,0:T(8,128)(2,1)S(1)} all-to-all(bf16[4,64,1024]{2,1,0:T(8,128)(2,1)S(1)} %bitcast.26), channel_id=1, replica_groups=mesh['gx'=64,'gy'=4] {'gy'}, dimensions={0} | all-to-all | bytes 1048576 | tf_op jit(solution)/shard_map/all_to_all | solution.py:205
  17.3 0.7 collective-permute-start.3
  18.0 0.7 collective-permute-start.2
  18.7 0.8 copies.4
  19.5 3.5 %all-to-all-start.1 = ((bf16[4,64,1024]{2,1,0:T(8,128)(2,1)}), bf16[4,64,1024]{2,1,0:T(8,128)(2,1)S(1)}, u32[]{:S(2)}, u32[]{:S(2)}) async-start(bf16[4,64,1024]{2,1,0:T(8,128)(2,1)} %bitcast.5), calls=%async_computation.1 | async-start | bytes 1048576 | tf_op jit(solution)/shard_map/all_to_all | solution.py:205
  23.0 2.7 %pick.5 = f32[256,1024]{1,0:T(8,128)} custom-call(f32[512,1024]{1,0:T(8,128)S(1)} %copy-done.1, s32[64,256]{1,0:T(8,128)S(1)} %copy-done.15, s32[1,3]{1,0:T(1,128)S(1)} %add_bitcast_fusion.place), custom_call_target="tpu_custom_call" | custom-call | flops 805306368 | bytes 3211276 | tf_op jit(solution)/shard_map/pick/pallas_call | solution.py:23
  25.7 5.4 %all-to-all-done.1 = bf16[4,64,1024]{2,1,0:T(8,128)(2,1)S(1)} async-done(((bf16[4,64,1024]{2,1,0:T(8,128)(2,1)}), bf16[4,64,1024]{2,1,0:T(8,128)(2,1)S(1)}, u32[]{:S(2)}, u32[]{:S(2)}) %all-to-all-start.1) | async-done | bytes 524320 | tf_op jit(solution)/shard_map/all_to_all | solution.py:205
  31.0 4.2 %all-to-all-start.2 = ((f32[4,64,1024]{2,1,0:T(8,128)}), f32[4,64,1024]{2,1,0:T(8,128)}, u32[]{:S(2)}, u32[]{:S(2)}) async-start(f32[4,64,1024]{2,1,0:T(8,128)} %bitcast.7), calls=%async_computation.2 | async-start | bytes 2097152 | tf_op jit(solution)/shard_map/all_to_all | solution.py:205
  35.3 10.1 %collective-permute-start.1 = (f32[1,256]{1,0:T(1,128)S(1)}, f32[1,256]{1,0:T(1,128)S(1)}, u32[]{:S(2)}, u32[]{:S(2)}) collective-permute-start(f32[1,256]{1,0:T(1,128)S(1)} %copy-done.18), channel_id=1, source_target_pairs={{0,252},{1,253},{2,254},{3,255},{4,0},{5,1},{6,2},{7,3},{8,4},{9,5... | collective-permute-start | bytes 3080 | tf_op jit(solution)/shard_map/ppermute | solution.py:200
  45.4 0.1 copy.6.levels
  45.5 1.2 collective-permute-done.1.right
  46.6 7.2 %collective-permute-done.left = f32[1,256]{1,0:T(1,128)S(1)} collective-permute-done((f32[1,256]{1,0:T(1,128)S(1)}, f32[1,256]{1,0:T(1,128)S(1)}, u32[]{:S(2)}, u32[]{:S(2)}) %collective-permute-start) | collective-permute-done | bytes 1056 | tf_op jit(solution)/shard_map/ppermute | solution.py:200
  53.9 1.7 setup.1
  55.6 8.2 %root.4.refs_0_ = bf16[256,1024]{1,0:T(8,128)(2,1)S(1)} custom-call(bf16[256,1024]{1,0:T(8,128)(2,1)S(1)} %bitcast.27, f32[1,256]{1,0:T(1,128)S(1)} %get-tuple-element.41.variance), custom_call_target="tpu_custom_call" | custom-call | flops 8000000000 | bytes 1049600 | tf_op jit(solution)/shard_map/root/pallas_call | solution.py:23
  63.8 1.8 rows.3.own
  65.6 1.9 %collective-permute-start.5 = (bf16[64,1024]{1,0:T(8,128)(2,1)S(1)}, bf16[64,1024]{1,0:T(8,128)(2,1)S(1)}, u32[]{:S(2)}, u32[]{:S(2)}) collective-permute-start(bf16[64,1024]{1,0:T(8,128)(2,1)S(1)} %rows.3.own), channel_id=1, source_target_pairs={{0,8},{1,9},{2,10},{3,11},{4,0},{5,1},{6,2},{7,3},{8,4},{9,5},{10,... | collective-permute-start | bytes 393224 | tf_op jit(solution)/shard_map/ppermute | solution.py:200
  67.5 6.9 %collective-permute-start.4 = (bf16[64,1024]{1,0:T(8,128)(2,1)S(1)}, bf16[64,1024]{1,0:T(8,128)(2,1)S(1)}, u32[]{:S(2)}, u32[]{:S(2)}) collective-permute-start(bf16[64,1024]{1,0:T(8,128)(2,1)S(1)} %rows.3.own), channel_id=1, source_target_pairs={{0,4},{1,5},{2,6},{3,7},{4,8},{5,9},{6,10},{7,11},{8,0},{9,1},{10,... | collective-permute-start | bytes 393224 | tf_op jit(solution)/shard_map/ppermute | solution.py:200
  74.5 1.0 collective-permute-done.5.second
  75.5 1.7 collective-permute-done.4.first
  77.2 0.8 copies.5
  78.0 4.6 %all-to-all-start.3 = ((bf16[4,64,1024]{2,1,0:T(8,128)(2,1)}), bf16[4,64,1024]{2,1,0:T(8,128)(2,1)S(1)}, u32[]{:S(2)}, u32[]{:S(2)}) async-start(bf16[4,64,1024]{2,1,0:T(8,128)(2,1)} %bitcast.9), calls=%async_computation.3 | async-start | bytes 1048576 | tf_op jit(solution)/shard_map/all_to_all | solution.py:205
  82.6 1.7 pick.6
  84.3 1.0 copy-done.9
  85.3 5.4 %all-to-all-done.3 = bf16[4,64,1024]{2,1,0:T(8,128)(2,1)S(1)} async-done(((bf16[4,64,1024]{2,1,0:T(8,128)(2,1)}), bf16[4,64,1024]{2,1,0:T(8,128)(2,1)S(1)}, u32[]{:S(2)}, u32[]{:S(2)}) %all-to-all-start.3) | async-done | bytes 524320 | tf_op jit(solution)/shard_map/all_to_all | solution.py:205
  90.7 4.3 %all-to-all-start.4 = ((f32[4,64,1024]{2,1,0:T(8,128)}), f32[4,64,1024]{2,1,0:T(8,128)}, u32[]{:S(2)}, u32[]{:S(2)}) async-start(f32[4,64,1024]{2,1,0:T(8,128)} %bitcast.23), calls=%async_computation.4 | async-start | bytes 2097152 | tf_op jit(solution)/shard_map/all_to_all | solution.py:205
  95.0 1.8 tile.4.parts
  96.8 0.0 copy-start.2
  96.8 1.3 copy-done.2
  98.1 1.0 copy-done.17
  99.2 8.2 %root.5.refs_0_.refs_2_ = bf16[256,1024]{1,0:T(8,128)(2,1)S(1)} custom-call(bf16[256,1024]{1,0:T(8,128)(2,1)S(1)} %bitcast.28, f32[1,256]{1,0:T(1,128)S(1)} %get-tuple-element.47.variance), custom_call_target="tpu_custom_call" | custom-call | flops 8000000000 | bytes 1049600 | tf_op jit(solution)/shard_map/root/pallas_call | solution.py:23
  107.3 2.4 %rows.4.own = bf16[64,1024]{1,0:T(8,128)(2,1)S(1)} custom-call(f32[256,1024]{1,0:T(8,128)} %bitcast.12.parts, bf16[256,1024]{1,0:T(8,128)(2,1)S(1)} %root.4.refs_0_, f32[64,1]{1,0:T(8,128)S(1)} %get-tuple-element.51.refs_1_, bf16[256,1024]{1,0:T(8,128)(2,1)S(1)} %root.5.refs_0_.refs_2_, f32[64,1]{1,0:T(8,128)S(1)} %get-tuple-element.52.refs_3_), custom_call_target="tpu_custom_call" | custom-call | flops 134217728 | bytes 2228736 | tf_op jit(solution)/shard_map/rows/pallas_call | solution.py:23
  109.7 1.9 %collective-permute-start.7 = (bf16[64,1024]{1,0:T(8,128)(2,1)S(1)}, bf16[64,1024]{1,0:T(8,128)(2,1)S(1)}, u32[]{:S(2)}, u32[]{:S(2)}) collective-permute-start(bf16[64,1024]{1,0:T(8,128)(2,1)S(1)} %rows.4.own), channel_id=1, source_target_pairs={{4,12},{5,13},{6,14},{7,15},{8,4},{9,5},{10,6},{11,7},{12,8},{13,9... | collective-permute-start | bytes 393224 | tf_op jit(solution)/shard_map/ppermute | solution.py:200
  111.6 2.4 %collective-permute-start.6 = (bf16[64,1024]{1,0:T(8,128)(2,1)S(1)}, bf16[64,1024]{1,0:T(8,128)(2,1)S(1)}, u32[]{:S(2)}, u32[]{:S(2)}) collective-permute-start(bf16[64,1024]{1,0:T(8,128)(2,1)S(1)} %rows.4.own), channel_id=1, source_target_pairs={{4,8},{5,9},{6,10},{7,11},{8,12},{9,13},{10,14},{11,15},{12,4},{13... | collective-permute-start | bytes 393224 | tf_op jit(solution)/shard_map/ppermute | solution.py:200
  114.1 0.1 collective-permute-done.7.second
  114.1 3.8 %collective-permute-done.6.first = bf16[64,1024]{1,0:T(8,128)(2,1)S(1)} collective-permute-done((bf16[64,1024]{1,0:T(8,128)(2,1)S(1)}, bf16[64,1024]{1,0:T(8,128)(2,1)S(1)}, u32[]{:S(2)}, u32[]{:S(2)}) %collective-permute-start.6) | collective-permute-done | bytes 131104 | tf_op jit(solution)/shard_map/ppermute | solution.py:200
  118.0 0.8 copy-done.10
  118.8 4.8 %all-to-all-start.5 = ((bf16[4,64,1024]{2,1,0:T(8,128)(2,1)}), bf16[4,64,1024]{2,1,0:T(8,128)(2,1)}, u32[]{:S(2)}, u32[]{:S(2)}) async-start(bf16[4,64,1024]{2,1,0:T(8,128)(2,1)} %bitcast.24), calls=%async_computation.5 | async-start | bytes 1048576 | tf_op jit(solution)/shard_map/all_to_all | solution.py:205
  123.5 1.7 pick.7
  125.2 1.0 copy-done.8
  126.2 5.5 %all-to-all-done.5 = bf16[4,64,1024]{2,1,0:T(8,128)(2,1)} async-done(((bf16[4,64,1024]{2,1,0:T(8,128)(2,1)}), bf16[4,64,1024]{2,1,0:T(8,128)(2,1)}, u32[]{:S(2)}, u32[]{:S(2)}) %all-to-all-start.5) | async-done | bytes 524320 | tf_op jit(solution)/shard_map/all_to_all | solution.py:205
  131.7 4.4 %all-to-all-start.6 = ((f32[4,64,1024]{2,1,0:T(8,128)}), f32[4,64,1024]{2,1,0:T(8,128)}, u32[]{:S(2)}, u32[]{:S(2)}) async-start(f32[4,64,1024]{2,1,0:T(8,128)} %bitcast.22), calls=%async_computation.6 | async-start | bytes 2097152 | tf_op jit(solution)/shard_map/all_to_all | solution.py:205
  136.2 1.9 tile.5.parts
  138.1 0.0 copy-start.4
  138.1 1.3 copy-done.4
  139.4 9.2 %root.6.refs_0_.refs_4_ = bf16[256,1024]{1,0:T(8,128)(2,1)S(1)} custom-call(bf16[256,1024]{1,0:T(8,128)(2,1)} %bitcast.14.pieces, f32[1,256]{1,0:T(1,128)S(1)} %get-tuple-element.54.variance), custom_call_target="tpu_custom_call" | custom-call | flops 8000000000 | bytes 1049600 | tf_op jit(solution)/shard_map/root/pallas_call | solution.py:23
  148.6 0.8 copy-done.11
  149.4 1.0 copy-done.12
  150.5 3.0 %rows.5.own = bf16[64,1024]{1,0:T(8,128)(2,1)S(1)} custom-call(f32[256,1024]{1,0:T(8,128)} %bitcast.16.parts, bf16[256,1024]{1,0:T(8,128)(2,1)S(1)} %root.4.refs_0_, f32[64,1]{1,0:T(8,128)S(1)} %get-tuple-element.58.refs_1_, bf16[256,1024]{1,0:T(8,128)(2,1)S(1)} %root.5.refs_0_.refs_2_, f32[64,1]{1,0:T(8,128)S(1)} %get-tuple-element.59.refs_3_, ...), custom_call_target="tpu_custom_call" | custom-call | flops 201326592 | bytes 2753280 | tf_op jit(solution)/shard_map/rows/pallas_call | solution.py:23
  153.4 2.1 %collective-permute-start.9 = (bf16[64,1024]{1,0:T(8,128)(2,1)S(1)}, bf16[64,1024]{1,0:T(8,128)(2,1)S(1)}, u32[]{:S(2)}, u32[]{:S(2)}) collective-permute-start(bf16[64,1024]{1,0:T(8,128)(2,1)S(1)} %rows.5.own), channel_id=1, source_target_pairs={{8,16},{9,17},{10,18},{11,19},{12,8},{13,9},{14,10},{15,11},{16,12... | collective-permute-start | bytes 393224 | tf_op jit(solution)/shard_map/ppermute | solution.py:200
  155.5 2.4 %collective-permute-start.8 = (bf16[64,1024]{1,0:T(8,128)(2,1)S(1)}, bf16[64,1024]{1,0:T(8,128)(2,1)S(1)}, u32[]{:S(2)}, u32[]{:S(2)}) collective-permute-start(bf16[64,1024]{1,0:T(8,128)(2,1)S(1)} %rows.5.own), channel_id=1, source_target_pairs={{8,12},{9,13},{10,14},{11,15},{12,16},{13,17},{14,18},{15,19},{16,... | collective-permute-start | bytes 393224 | tf_op jit(solution)/shard_map/ppermute | solution.py:200
  157.9 0.1 collective-permute-done.9.second
  158.0 4.4 %collective-permute-done.8.first = bf16[64,1024]{1,0:T(8,128)(2,1)S(1)} collective-permute-done((bf16[64,1024]{1,0:T(8,128)(2,1)S(1)}, bf16[64,1024]{1,0:T(8,128)(2,1)S(1)}, u32[]{:S(2)}, u32[]{:S(2)}) %collective-permute-start.8) | collective-permute-done | bytes 131104 | tf_op jit(solution)/shard_map/ppermute | solution.py:200
  162.4 0.8 copies.7
  163.2 4.6 %all-to-all-start.7 = ((bf16[4,64,1024]{2,1,0:T(8,128)(2,1)}), bf16[4,64,1024]{2,1,0:T(8,128)(2,1)S(1)}, u32[]{:S(2)}, u32[]{:S(2)}) async-start(bf16[4,64,1024]{2,1,0:T(8,128)(2,1)} %bitcast.17), calls=%async_computation.7 | async-start | bytes 1048576 | tf_op jit(solution)/shard_map/all_to_all | solution.py:205
  167.8 1.9 tile.6.parts
  169.6 1.3 copy-done.6
  171.0 4.9 %all-to-all-done.7 = bf16[4,64,1024]{2,1,0:T(8,128)(2,1)S(1)} async-done(((bf16[4,64,1024]{2,1,0:T(8,128)(2,1)}), bf16[4,64,1024]{2,1,0:T(8,128)(2,1)S(1)}, u32[]{:S(2)}, u32[]{:S(2)}) %all-to-all-start.7) | async-done | bytes 524320 | tf_op jit(solution)/shard_map/all_to_all | solution.py:205
  175.8 8.2 %root.7.refs_0_ = bf16[256,1024]{1,0:T(8,128)(2,1)S(1)} custom-call(bf16[256,1024]{1,0:T(8,128)(2,1)S(1)} %bitcast.29, f32[1,256]{1,0:T(1,128)S(1)} %get-tuple-element.61.variance), custom_call_target="tpu_custom_call" | custom-call | flops 8000000000 | bytes 1049600 | tf_op jit(solution)/shard_map/root/pallas_call | solution.py:23
  184.0 3.2 %tile.7 = f32[512,1024]{1,0:T(8,128)} custom-call(f32[512,1024]{1,0:T(8,128)S(1)} %copy-done.7, bf16[256,1024]{1,0:T(8,128)(2,1)S(1)} %root.7.refs_0_, f32[1,1]{1,0:T(1,128)} %get-tuple-element.62.refs_1_), custom_call_target="tpu_custom_call" | custom-call | flops 536870912 | bytes 4718596 | tf_op jit(solution)/shard_map/tile/pallas_call | solution.py:23
  (35 shorter events, 0.1 us)
Async XLA Ops:
  0.1 1.6 copy-start
  1.7 0.8 copy-start.14
  3.5 19.4 %copy-start.1 = (f32[512,1024]{1,0:T(8,128)S(1)}, f32[512,1024]{1,0:T(8,128)}, u32[]{:S(2)}) copy-start(f32[512,1024]{1,0:T(8,128)} %state.7) | copy-start | bytes 6291460
  3.5 19.4 %copy-start.15 = (s32[64,256]{1,0:T(8,128)S(1)}, s32[64,256]{1,0:T(8,128)}, u32[]{:S(2)}) copy-start(s32[64,256]{1,0:T(8,128)} %obs.9) | copy-start | bytes 196612
  17.3 1.4 collective-permute-start.3
  18.0 0.7 collective-permute-start.2
  19.5 11.5 %all-to-all-start.1 = ((bf16[4,64,1024]{2,1,0:T(8,128)(2,1)}), bf16[4,64,1024]{2,1,0:T(8,128)(2,1)S(1)}, u32[]{:S(2)}, u32[]{:S(2)}) async-start(bf16[4,64,1024]{2,1,0:T(8,128)(2,1)} %bitcast.5), calls=%async_computation.1 | async-start | bytes 1048576 | tf_op jit(solution)/shard_map/all_to_all | solution.py:205
  23.0 12.3 %copy-start.18 = (f32[1,256]{1,0:T(1,128)S(1)}, f32[1,256]{1,0:T(1,128)}, u32[]{:S(2)}) copy-start(f32[1,256]{1,0:T(1,128)} %own.1) | copy-start | bytes 3076
  23.0 22.3 %copy-start.19 = (s32[64,3,4]{0,2,1:T(4,128)S(1)}, s32[64,3,4]{0,2,1:T(4,128)}, u32[]{:S(2)}) copy-start(s32[64,3,4]{0,2,1:T(4,128)} %param.7) | copy-start | bytes 9220
  31.0 32.8 %all-to-all-start.2 = ((f32[4,64,1024]{2,1,0:T(8,128)}), f32[4,64,1024]{2,1,0:T(8,128)}, u32[]{:S(2)}, u32[]{:S(2)}) async-start(f32[4,64,1024]{2,1,0:T(8,128)} %bitcast.7), calls=%async_computation.2 | async-start | bytes 2097152 | tf_op jit(solution)/shard_map/all_to_all | solution.py:205
  35.3 11.4 %collective-permute-start.1 = (f32[1,256]{1,0:T(1,128)S(1)}, f32[1,256]{1,0:T(1,128)S(1)}, u32[]{:S(2)}, u32[]{:S(2)}) collective-permute-start(f32[1,256]{1,0:T(1,128)S(1)} %copy-done.18), channel_id=1, source_target_pairs={{0,252},{1,253},{2,254},{3,255},{4,0},{5,1},{6,2},{7,3},{8,4},{9,5... | collective-permute-start | bytes 3080 | tf_op jit(solution)/shard_map/ppermute | solution.py:200
  45.3 8.5 %collective-permute-start = (f32[1,256]{1,0:T(1,128)S(1)}, f32[1,256]{1,0:T(1,128)S(1)}, u32[]{:S(2)}, u32[]{:S(2)}) collective-permute-start(f32[1,256]{1,0:T(1,128)S(1)} %copy-done.18), channel_id=1, source_target_pairs={{0,4},{1,5},{2,6},{3,7},{4,8},{5,9},{6,10},{7,11},{8,12},{9,13},{1... | collective-permute-start | bytes 3080 | tf_op jit(solution)/shard_map/ppermute | solution.py:200
  65.6 9.9 %collective-permute-start.5 = (bf16[64,1024]{1,0:T(8,128)(2,1)S(1)}, bf16[64,1024]{1,0:T(8,128)(2,1)S(1)}, u32[]{:S(2)}, u32[]{:S(2)}) collective-permute-start(bf16[64,1024]{1,0:T(8,128)(2,1)S(1)} %rows.3.own), channel_id=1, source_target_pairs={{0,8},{1,9},{2,10},{3,11},{4,0},{5,1},{6,2},{7,3},{8,4},{9,5},{10,... | collective-permute-start | bytes 393224 | tf_op jit(solution)/shard_map/ppermute | solution.py:200
  67.5 9.7 %collective-permute-start.4 = (bf16[64,1024]{1,0:T(8,128)(2,1)S(1)}, bf16[64,1024]{1,0:T(8,128)(2,1)S(1)}, u32[]{:S(2)}, u32[]{:S(2)}) collective-permute-start(bf16[64,1024]{1,0:T(8,128)(2,1)S(1)} %rows.3.own), channel_id=1, source_target_pairs={{0,4},{1,5},{2,6},{3,7},{4,8},{5,9},{6,10},{7,11},{8,0},{9,1},{10,... | collective-permute-start | bytes 393224 | tf_op jit(solution)/shard_map/ppermute | solution.py:200
  78.0 12.7 %all-to-all-start.3 = ((bf16[4,64,1024]{2,1,0:T(8,128)(2,1)}), bf16[4,64,1024]{2,1,0:T(8,128)(2,1)S(1)}, u32[]{:S(2)}, u32[]{:S(2)}) async-start(bf16[4,64,1024]{2,1,0:T(8,128)(2,1)} %bitcast.9), calls=%async_computation.3 | async-start | bytes 1048576 | tf_op jit(solution)/shard_map/all_to_all | solution.py:205
  84.3 1.0 copy-start.9
  90.7 6.1 %copy-start.16 = (bf16[4,64,1024]{2,1,0:T(8,128)(2,1)}, bf16[4,64,1024]{2,1,0:T(8,128)(2,1)S(1)}, u32[]{:S(2)}) copy-start(bf16[4,64,1024]{2,1,0:T(8,128)(2,1)S(1)} %all-to-all-done.3) | copy-start | bytes 1572868
  90.7 16.6 %all-to-all-start.4 = ((f32[4,64,1024]{2,1,0:T(8,128)}), f32[4,64,1024]{2,1,0:T(8,128)}, u32[]{:S(2)}, u32[]{:S(2)}) async-start(f32[4,64,1024]{2,1,0:T(8,128)} %bitcast.23), calls=%async_computation.4 | async-start | bytes 2097152 | tf_op jit(solution)/shard_map/all_to_all | solution.py:205
  96.8 1.3 copy-start.2
  98.1 1.0 copy-start.17
  109.7 4.4 %collective-permute-start.7 = (bf16[64,1024]{1,0:T(8,128)(2,1)S(1)}, bf16[64,1024]{1,0:T(8,128)(2,1)S(1)}, u32[]{:S(2)}, u32[]{:S(2)}) collective-permute-start(bf16[64,1024]{1,0:T(8,128)(2,1)S(1)} %rows.4.own), channel_id=1, source_target_pairs={{4,12},{5,13},{6,14},{7,15},{8,4},{9,5},{10,6},{11,7},{12,8},{13,9... | collective-permute-start | bytes 393224 | tf_op jit(solution)/shard_map/ppermute | solution.py:200
  111.6 6.3 %collective-permute-start.6 = (bf16[64,1024]{1,0:T(8,128)(2,1)S(1)}, bf16[64,1024]{1,0:T(8,128)(2,1)S(1)}, u32[]{:S(2)}, u32[]{:S(2)}) collective-permute-start(bf16[64,1024]{1,0:T(8,128)(2,1)S(1)} %rows.4.own), channel_id=1, source_target_pairs={{4,8},{5,9},{6,10},{7,11},{8,12},{9,13},{10,14},{11,15},{12,4},{13... | collective-permute-start | bytes 393224 | tf_op jit(solution)/shard_map/ppermute | solution.py:200
  118.0 0.8 copy-start.10
  118.8 12.9 %all-to-all-start.5 = ((bf16[4,64,1024]{2,1,0:T(8,128)(2,1)}), bf16[4,64,1024]{2,1,0:T(8,128)(2,1)}, u32[]{:S(2)}, u32[]{:S(2)}) async-start(bf16[4,64,1024]{2,1,0:T(8,128)(2,1)} %bitcast.24), calls=%async_computation.5 | async-start | bytes 1048576 | tf_op jit(solution)/shard_map/all_to_all | solution.py:205
  125.2 1.0 copy-start.8
  126.2 10.0 %copy-start.3 = (f32[512,1024]{1,0:T(8,128)S(1)}, f32[512,1024]{1,0:T(8,128)}, u32[]{:S(2)}) copy-start(f32[512,1024]{1,0:T(8,128)} %copy-done.2) | copy-start | bytes 6291460
  131.7 17.7 %all-to-all-start.6 = ((f32[4,64,1024]{2,1,0:T(8,128)}), f32[4,64,1024]{2,1,0:T(8,128)}, u32[]{:S(2)}, u32[]{:S(2)}) async-start(f32[4,64,1024]{2,1,0:T(8,128)} %bitcast.22), calls=%async_computation.6 | async-start | bytes 2097152 | tf_op jit(solution)/shard_map/all_to_all | solution.py:205
  138.1 1.3 copy-start.4
  148.6 0.8 copy-start.11
  149.4 1.0 copy-start.12
  150.4 17.3 %copy-start.5 = (f32[512,1024]{1,0:T(8,128)S(1)}, f32[512,1024]{1,0:T(8,128)}, u32[]{:S(2)}) copy-start(f32[512,1024]{1,0:T(8,128)} %copy-done.4) | copy-start | bytes 6291460
  153.4 14.3 %copy-start.13 = (bf16[256,1024]{1,0:T(8,128)(2,1)S(1)}, bf16[256,1024]{1,0:T(8,128)(2,1)}, u32[]{:S(2)}) copy-start(bf16[256,1024]{1,0:T(8,128)(2,1)} %copy-done.11) | copy-start | bytes 1572868
  153.4 4.6 %collective-permute-start.9 = (bf16[64,1024]{1,0:T(8,128)(2,1)S(1)}, bf16[64,1024]{1,0:T(8,128)(2,1)S(1)}, u32[]{:S(2)}, u32[]{:S(2)}) collective-permute-start(bf16[64,1024]{1,0:T(8,128)(2,1)S(1)} %rows.5.own), channel_id=1, source_target_pairs={{8,16},{9,17},{10,18},{11,19},{12,8},{13,9},{14,10},{15,11},{16,12... | collective-permute-start | bytes 393224 | tf_op jit(solution)/shard_map/ppermute | solution.py:200
  155.5 6.9 %collective-permute-start.8 = (bf16[64,1024]{1,0:T(8,128)(2,1)S(1)}, bf16[64,1024]{1,0:T(8,128)(2,1)S(1)}, u32[]{:S(2)}, u32[]{:S(2)}) collective-permute-start(bf16[64,1024]{1,0:T(8,128)(2,1)S(1)} %rows.5.own), channel_id=1, source_target_pairs={{8,12},{9,13},{10,14},{11,15},{12,16},{13,17},{14,18},{15,19},{16,... | collective-permute-start | bytes 393224 | tf_op jit(solution)/shard_map/ppermute | solution.py:200
  163.2 12.6 %all-to-all-start.7 = ((bf16[4,64,1024]{2,1,0:T(8,128)(2,1)}), bf16[4,64,1024]{2,1,0:T(8,128)(2,1)S(1)}, u32[]{:S(2)}, u32[]{:S(2)}) async-start(bf16[4,64,1024]{2,1,0:T(8,128)(2,1)} %bitcast.17), calls=%async_computation.7 | async-start | bytes 1048576 | tf_op jit(solution)/shard_map/all_to_all | solution.py:205
  169.6 1.3 copy-start.6
  175.8 8.2 %copy-start.7 = (f32[512,1024]{1,0:T(8,128)S(1)}, f32[512,1024]{1,0:T(8,128)}, u32[]{:S(2)}) copy-start(f32[512,1024]{1,0:T(8,128)} %copy-done.6) | copy-start | bytes 6291460

commit v2 on v1

--- a/solution.py
+++ b/solution.py
@@ -16,7 +16,7 @@
 BF16 = jnp.bfloat16
 
 
-def kernel_call(body, out, args, name, flops, smem=()):
+def kernel_call(body, out, args, name, flops, smem=(), scratch=()):
     whole = pl.BlockSpec(memory_space=pltpu.VMEM)
     scalar = pl.BlockSpec(memory_space=pltpu.SMEM)
     leaves = [*args, *jax.tree.leaves(out)]
@@ -25,6 +25,7 @@
         out_shape=out,
         in_specs=[scalar if n in smem else whole for n in range(len(args))],
         out_specs=jax.tree.map(lambda _: whole, out),
+        scratch_shapes=scratch,
         name=name,
         interpret=INTERPRET,
         cost_estimate=pl.CostEstimate(
@@ -46,12 +47,6 @@
     )
 
 
-def dot_tn(left, right):
-    return lax.dot_general(
-        left, right, (((0,), (0,)), ((), ())), preferred_element_type=F32
-    )
-
-
 def halves(value):
     high = value.astype(BF16)
     return high, (value - high.astype(F32)).astype(BF16)
@@ -67,30 +62,38 @@
     return slot, offset != 2, lax.rem(col - slot + 1 + columns, columns)
 
 
-def pick_kernel(tiles, colours, state, obs, place, out):
+def pick_kernel(colours, state, obs, place, *refs):
+    outs, scratch = refs[:-1], refs[-1]
+    tiles = len(outs)
     tile_rows = state.shape[0]
     columns, size = obs.shape
     share = size // tiles
     col, tile = place[0, 0], place[0, 1]
-    rest = state[...]
-    parts = [rest.astype(BF16)]
-    if out.dtype == F32:
-        rest = rest - parts[0].astype(F32)
-        parts.append(rest.astype(BF16))
-        parts.append((rest - parts[1].astype(F32)).astype(BF16))
+    band = state.shape[1] // tiles
     for n, colour in enumerate(colours):
         slot, active, batch = standing(col, colour, columns)
         first = jnp.where(active, (slot * tiles + tile) * tile_rows, -(1 << 20))
         local = obs[pl.ds(batch, 1), :] - first
         spots = lax.broadcasted_iota(jnp.int32, (tile_rows, size), 0)
-        chosen = jnp.where(spots == local, 1.0, 0.0).astype(BF16)
-        picked = dot_tn(chosen, parts[0])
-        for part in parts[1:]:
-            picked = picked + dot_tn(chosen, part)
-        picked = picked.astype(out.dtype)
-        for m in range(tiles):
-            start = (m * len(colours) + n) * share
-            out[start : start + share, :] = picked[m * share : (m + 1) * share]
+        chosen = jnp.where(spots == local, 1.0, 0.0).T.astype(BF16)
+
+        def pick_band(m, _):
+            lanes = pl.ds(pl.multiple_of(m * band, band), band)
+            rest = state[:, lanes]
+            high = rest.astype(BF16)
+            picked = dot(chosen, high)
+            if scratch.dtype == F32:
+                rest = rest - high.astype(F32)
+                middle = rest.astype(BF16)
+                picked = picked + dot(chosen, middle)
+                picked = picked + dot(chosen, (rest - middle.astype(F32)).astype(BF16))
+            scratch[:, lanes] = picked.astype(scratch.dtype)
+            return 0
+
+        lax.fori_loop(0, tiles, pick_band, 0)
+        for step, out in enumerate(outs):
+            start = pl.multiple_of(lax.rem(tile + step, tiles) * share, share)
+            out[n * share : (n + 1) * share, :] = scratch[pl.ds(start, share), :]
 
 
 def setup_kernel(pairs, tiles, tile_rows, obs, levels, place, own, left, right, *outs):
@@ -122,11 +125,20 @@
         value = jnp.where(
             active & (slot == 2), left[...], jnp.where(active & (slot == 0), right[...], own[...])
         )
-        outs[len(pairs) + NCOL + colour][...] = value
-
-
-def root_kernel(pieces, variance, out):
-    observed = pieces[...]
+        pieces = [value[:, n * share : (n + 1) * share] for n in range(tiles)]
+        ordered = []
+        for step in range(tiles):
+            source = lax.rem(tile + tiles - step, tiles)
+            piece = pieces[0]
+            for n in range(1, tiles):
+                piece = jnp.where(source == n, pieces[n], piece)
+            ordered.append(piece)
+        outs[len(pairs) + NCOL + colour][...] = jnp.concatenate(ordered, axis=1)
+
+
+def root_kernel(*refs):
+    *pieces, variance, out = refs
+    observed = jnp.concatenate([piece[...] for piece in pieces], axis=0)
     size, members = observed.shape
     row = lax.broadcasted_iota(jnp.int32, (size, size), 0)
     column = lax.broadcasted_iota(jnp.int32, (size, size), 1)
@@ -151,17 +163,17 @@
     out[...] = dot(inverse_half, observed).astype(BF16)
 
 
-def summed(parts, count):
-    rows = parts.shape[0] // count
-    total = parts[:rows, :]
-    for n in range(1, count):
-        total = total + parts[n * rows : (n + 1) * rows, :]
+def summed(parts):
+    total = parts[0][...]
+    for part in parts[1:]:
+        total = total + part[...]
     return total
 
 
-def rows_kernel(count, parts, *refs):
-    *pairs, out = refs
-    rows = summed(parts, count)
+def rows_kernel(count, which, *refs):
+    *pairs, out = refs[count:]
+    share = out.shape[0]
+    rows = summed([ref.at[which * share : (which + 1) * share, :] for ref in refs[:count]])
     for transformed, factor in zip(pairs[::2], pairs[1::2]):
         source = transformed[...]
         projected = dot_nt(rows.astype(BF16), source).astype(BF16)
@@ -169,15 +181,16 @@
     out[...] = rows.astype(out.dtype)
 
 
-def sum_kernel(count, parts, out):
-    out[...] = summed(parts, count)
-
-
-def copies_kernel(own, first, second, out):
-    total = (own[...] + first[...]) + second[...]
-    rows = total.shape[0]
-    for n in range(out.shape[0] // rows):
-        out[n * rows : (n + 1) * rows, :] = total
+def tile_kernel(state, transformed, factor, out):
+    value = state[...]
+    source = transformed[...]
+    projected = dot_nt(value.astype(BF16), source).astype(BF16)
+    out[...] = value - factor[...] * dot(projected, source)
+
+
+def sum_kernel(*refs):
+    *parts, out = refs
+    out[...] = summed(parts)
 
 
 def on_device(anomalies, obs_rows, obs_var, taper_level):
@@ -199,10 +212,8 @@
         ]
         return lax.ppermute(value, AXES, flat)
 
-    def over_gy(value):
-        rows = value.shape[0]
-        parts = value.reshape(tiles, rows // tiles, members)
-        return lax.all_to_all(parts, "gy", 0, 0, tiled=True).reshape(rows, members)
+    def along_gy(value, step):
+        return hop(value, [((c, n), (c, n + step)) for c in everywhere for n in range(tiles)])
 
     def along_gx(value, colour, step):
         trio = (-1, 0, 1)
@@ -212,64 +223,80 @@
             for m in range(3)
             for n in range(tiles)
         ]
+        pairs += [
+            ((b + 2, n), (b + 2, n + 1 - 2 * (n % 2)))
+            for b in range(colour, columns, NCOL)
+            for n in range(tiles)
+        ]
         return hop(value, pairs)
 
     def beside(value, step):
         return hop(value, [((c, n), (c + step, n)) for c in everywhere for n in range(tiles)])
 
     def pick(colours, dtype, state):
+        shape = jax.ShapeDtypeStruct((len(colours) * share, members), dtype)
         return kernel_call(
-            functools.partial(pick_kernel, tiles, colours),
-            jax.ShapeDtypeStruct((len(colours) * size, members), dtype),
+            functools.partial(pick_kernel, colours),
+            [shape] * tiles,
             [state, obs_rows, place],
             "pick",
             2 * size * tile_rows * members * len(colours) * (1 if dtype == BF16 else 3),
             smem=(2,),
-        )
+            scratch=[pltpu.VMEM((size, members), dtype)],
+        )
+
+    def scattered(parts):
+        return [parts[0], *[along_gy(parts[n], n) for n in range(1, tiles)]]
+
+    def added(parts):
+        shape = jax.ShapeDtypeStruct(parts[0].shape, parts[0].dtype)
+        return kernel_call(sum_kernel, shape, parts, "sum", 1_000_000)
 
     def collected(rows, colour):
-        args = [rows, along_gx(rows, colour, 1), along_gx(rows, colour, 2)]
-        shape = jax.ShapeDtypeStruct((size, members), BF16)
-        return over_gy(kernel_call(copies_kernel, shape, args, "copies", 1_000_000))
+        first, second = (along_gx(rows, colour, step) for step in (1, 2))
+        whole = added([rows, first, second])
+        return [whole, *[along_gy(whole, step) for step in range(1, tiles)]]
 
     def transform(pieces, variance):
         return kernel_call(
             root_kernel,
             jax.ShapeDtypeStruct((size, members), BF16),
-            [pieces, variance],
+            [*pieces, variance],
             "root",
-            8_000_000_000,
-        )
-
-    def move(parts, count, sources, dtype, name="rows"):
-        rows = parts.shape[0] // count
+            1_000_000,
+        )
+
+    def move_tile(state, transformed, factor):
         return kernel_call(
-            functools.partial(rows_kernel, count),
+            tile_kernel,
+            jax.ShapeDtypeStruct(state.shape, F32),
+            [state, transformed, factor],
+            "tile",
+            4 * tile_rows * size * members,
+        )
+
+    def move(parts, which, sources, dtype):
+        rows = share
+        return kernel_call(
+            functools.partial(rows_kernel, len(parts), which),
             jax.ShapeDtypeStruct((rows, members), dtype),
-            [parts, *[ref for pair in sources for ref in pair]],
-            name,
+            [*parts, *[ref for pair in sources for ref in pair]],
+            "rows",
             4 * rows * size * members * len(sources),
         )
 
     together = lax.optimization_barrier
-    parts0 = over_gy(pick((0,), BF16, anomalies))
-    total0 = kernel_call(
-        functools.partial(sum_kernel, tiles),
-        jax.ShapeDtypeStruct((share, members), BF16),
-        [parts0],
-        "sum",
-        1_000_000,
-    )
-    picked = [None, *[pick((colour,), F32, anomalies) for colour in range(1, NCOL)]]
+    total0 = added(scattered(pick((0,), BF16, anomalies)))
+    later, total0 = together((pick(range(1, NCOL), F32, anomalies), total0))
+    parts = scattered(later)
 
     pairs = [((target,), source) for target in range(1, NCOL) for source in range(target)]
-    own_var, _ = together((obs_var, total0))
     prepared = kernel_call(
         functools.partial(setup_kernel, pairs, tiles, tile_rows),
         [jax.ShapeDtypeStruct((len(t) * share, 1), F32) for t, _ in pairs]
         + [jax.ShapeDtypeStruct((1, 1), F32)] * NCOL
         + [jax.ShapeDtypeStruct((1, size), F32)] * NCOL,
-        [obs_rows, levels, place, obs_var, beside(own_var, 1), beside(own_var, -1)],
+        [obs_rows, levels, place, obs_var, beside(obs_var, 1), beside(obs_var, -1)],
         "setup",
         1_000_000,
         smem=(1, 2),
@@ -283,16 +310,12 @@
     done = []
     for colour in range(NCOL):
         pieces = collected(rows, colour)
-        if colour < NCOL - 1:
-            coming, pieces = together((picked[colour + 1], pieces))
-            parts = over_gy(coming)
         var, state = together((variance[colour], state))
         done.append(transform(pieces, var))
-        state_factor = [(done[colour], tile_factor[colour])]
         if colour < NCOL - 1:
             sources = [(done[n], row_factor[colour + 1, n]) for n in range(colour + 1)]
-            rows = move(parts, tiles, sources, BF16)
-        state = move(state, 1, state_factor, F32, "tile")
+            rows = move(parts, colour, sources, BF16)
+        state = move_tile(state, done[colour], tile_factor[colour])
     return state
 
 

time: 188 us -> 166 us (0.88)
  the two profiles are of different devices: /device:TPU:8 before, /device:TPU:6 now
where the time goes in v2:
time: 166 us; the launch traced here: 165 us
  starting transfers between devices  66.6 us (40%)
  Pallas kernels  56.7 us (34%)
  waiting for transfers between devices  39.2 us (24%)
  local copies, waits for them, and re-layouts  2.55 us (2%)
    ppermute x28, starting transfers between devices, hop(): return lax.ppermute(value, AXES, flat)  66.6 us
    pallas_call x19, Pallas kernels, kernel_call(): pl.pallas_call(body, out_shape=out, in_specs=[scalar if n in smem else wh...  56.7 us
    ppermute x28, waiting for transfers between devices, hop(): return lax.ppermute(value, AXES, flat)  39.2 us
  transfers between devices with their start and end apart: 28, of which 20 were waited for; matrix products, arithmetic and copies ran while one was open for 0% of the time, Pallas kernels for 14%

profile of v2, /device:TPU:6, one launch (start us, length us, event | category | flops | bytes accessed | tf_op | source)
XLA Modules:
  0.0 165.3 jit_solution(12290210644561121435)
XLA Ops:
  0.0 0.1 add_bitcast_fusion.place
  0.1 1.6 copy-done
  1.7 0.8 copy-done.2
  2.5 1.7 %pick.3 = (bf16[64,1024]{1,0:T(8,128)(2,1)S(1)}, bf16[64,1024]{1,0:T(8,128)(2,1)S(1)}, bf16[64,1024]{1,0:T(8,128)(2,1)S(1)}, bf16[64,1024]{1,0:T(8,128)(2,1)S(1)}) custom-call(f32[512,1024]{1,0:T(8,128)S(1)} %copy-done, s32[64,256]{1,0:T(8,128)S(1)} %copy-done.2, s32[1,3]{1,0:T(1,128)S(1)} %add_bitcast_fusion.place), custom_call_target="tpu_custom_call" | custom-call | flops 268435456 | bytes 2686988 | tf_op jit(solution)/shard_map/pick/pallas_call | solution.py:23
  4.2 2.3 %collective-permute-start.2 = (bf16[64,1024]{1,0:T(8,128)(2,1)S(1)}, bf16[64,1024]{1,0:T(8,128)(2,1)S(1)}, u32[]{:S(2)}, u32[]{:S(2)}) collective-permute-start(bf16[64,1024]{1,0:T(8,128)(2,1)S(1)} %get-tuple-element.50), channel_id=1, source_target_pairs={{0,1},{1,2},{2,3},{3,0},{4,5},{5,6},{6,7},{7,4},{8,9},{9,10},{10,1... | collective-permute-start | bytes 393224 | tf_op jit(solution)/shard_map/ppermute | solution.py:213
  6.5 0.7 collective-permute-start.3
  7.2 0.3 collective-permute-start.4
  7.4 7.3 %pick.2 = (f32[192,1024]{1,0:T(8,128)S(1)}, f32[192,1024]{1,0:T(8,128)}, f32[192,1024]{1,0:T(8,128)}, f32[192,1024]{1,0:T(8,128)}) custom-call(f32[512,1024]{1,0:T(8,128)S(1)} %copy-done, s32[64,256]{1,0:T(8,128)S(1)} %copy-done.2, s32[1,3]{1,0:T(1,128)S(1)} %add_bitcast_fusion.place), custom_call_target="tpu_custom_call" | custom-call | flops 2415919104 | bytes 5308428 | tf_op jit(solution)/shard_map/pick/pallas_call | solution.py:23
  14.8 3.0 %collective-permute-start.10 = (f32[192,1024]{1,0:T(8,128)}, f32[192,1024]{1,0:T(8,128)S(1)}, u32[]{:S(2)}, u32[]{:S(2)}) collective-permute-start(f32[192,1024]{1,0:T(8,128)} %get-tuple-element.58), channel_id=1, source_target_pairs={{0,1},{1,2},{2,3},{3,0},{4,5},{5,6},{6,7},{7,4},{8,9},{9,10},{10,1... | collective-permute-start | bytes 2359304 | tf_op jit(solution)/shard_map/ppermute | solution.py:213
  17.8 1.6 collective-permute-start.11
  19.5 5.9 %collective-permute-start.6 = (bf16[64,1024]{1,0:T(8,128)(2,1)S(1)}, bf16[64,1024]{1,0:T(8,128)(2,1)S(1)}, u32[]{:S(2)}, u32[]{:S(2)}) collective-permute-start(bf16[64,1024]{1,0:T(8,128)(2,1)S(1)} %sum.5.refs_0_), channel_id=1, source_target_pairs={{252,4},{253,5},{254,6},{255,7},{0,252},{1,253},{2,254},{3,255},{4... | collective-permute-start | bytes 393224 | tf_op jit(solution)/shard_map/ppermute | solution.py:213
  25.3 3.3 %collective-permute-done.6.refs_2_ = bf16[64,1024]{1,0:T(8,128)(2,1)S(1)} collective-permute-done((bf16[64,1024]{1,0:T(8,128)(2,1)S(1)}, bf16[64,1024]{1,0:T(8,128)(2,1)S(1)}, u32[]{:S(2)}, u32[]{:S(2)}) %collective-permute-start.6) | collective-permute-done | bytes 131104 | tf_op jit(solution)/shard_map/ppermute | solution.py:213
  28.7 4.4 %collective-permute-done.5.refs_1_ = bf16[64,1024]{1,0:T(8,128)(2,1)S(1)} collective-permute-done((bf16[64,1024]{1,0:T(8,128)(2,1)S(1)}, bf16[64,1024]{1,0:T(8,128)(2,1)S(1)}, u32[]{:S(2)}, u32[]{:S(2)}) %collective-permute-start.5) | collective-permute-done | bytes 131104 | tf_op jit(solution)/shard_map/ppermute | solution.py:213
  33.1 2.1 %collective-permute-start.9 = (bf16[64,1024]{1,0:T(8,128)(2,1)S(1)}, bf16[64,1024]{1,0:T(8,128)(2,1)S(1)}, u32[]{:S(2)}, u32[]{:S(2)}) collective-permute-start(bf16[64,1024]{1,0:T(8,128)(2,1)S(1)} %sum.6.refs_0_), channel_id=1, source_target_pairs={{0,3},{1,0},{2,1},{3,2},{4,7},{5,4},{6,5},{7,6},{8,11},{9,8},{10,9... | collective-permute-start | bytes 393224 | tf_op jit(solution)/shard_map/ppermute | solution.py:213
  35.2 6.3 %collective-permute-done.left = f32[1,256]{1,0:T(1,128)S(1)} collective-permute-done((f32[1,256]{1,0:T(1,128)S(1)}, f32[1,256]{1,0:T(1,128)S(1)}, u32[]{:S(2)}, u32[]{:S(2)}) %collective-permute-start) | collective-permute-done | bytes 1056 | tf_op jit(solution)/shard_map/ppermute | solution.py:213
  41.5 25.4 %collective-permute-start.1 = (f32[1,256]{1,0:T(1,128)S(1)}, f32[1,256]{1,0:T(1,128)S(1)}, u32[]{:S(2)}, u32[]{:S(2)}) collective-permute-start(f32[1,256]{1,0:T(1,128)S(1)} %copy-done.4), channel_id=1, source_target_pairs={{0,252},{1,253},{2,254},{3,255},{4,0},{5,1},{6,2},{7,3},{8,4},{9,5... | collective-permute-start | bytes 3080 | tf_op jit(solution)/shard_map/ppermute | solution.py:213
  66.9 1.3 collective-permute-done.1.right
  68.2 3.1 %collective-permute-start.8 = (bf16[64,1024]{1,0:T(8,128)(2,1)S(1)}, bf16[64,1024]{1,0:T(8,128)(2,1)}, u32[]{:S(2)}, u32[]{:S(2)}) collective-permute-start(bf16[64,1024]{1,0:T(8,128)(2,1)S(1)} %sum.6.refs_0_), channel_id=1, source_target_pairs={{0,2},{1,3},{2,0},{3,1},{4,6},{5,7},{6,4},{7,5},{8,10},{9,11},{10,... | collective-permute-start | bytes 393224 | tf_op jit(solution)/shard_map/ppermute | solution.py:213
  71.3 0.2 collective-permute-start.7
  71.5 0.1 copy.6.levels
  71.6 1.9 %setup.1 = (f32[64,1]{1,0:T(8,128)S(1)}, f32[64,1]{1,0:T(8,128)S(1)}, f32[64,1]{1,0:T(8,128)S(1)}, f32[64,1]{1,0:T(8,128)S(1)}, f32[64,1]{1,0:T(8,128)S(1)}, /*i...) custom-call(s32[64,256]{1,0:T(8,128)S(1)} %copy-done.3, ...), custom_call_target="tpu_custom_call" | custom-call | flops 1000000 | bytes 77340 | tf_op jit(solution)/shard_map/setup/pallas_call | solution.py:23
  73.4 1.3 collective-permute-done.8.refs_2_
  74.8 1.6 collective-permute-done.7.refs_1_
  76.4 9.1 %root.4.transformed.refs_4_ = bf16[256,1024]{1,0:T(8,128)(2,1)S(1)} custom-call(bf16[64,1024]{1,0:T(8,128)(2,1)S(1)} %sum.6.refs_0_, bf16[64,1024]{1,0:T(8,128)(2,1)} %collective-permute-done.7.refs_1_, bf16[64,1024]{1,0:T(8,128)(2,1)} %collective-permute-done.8.refs_2_, bf16[64,1024]{1,0:T(8,128)(2,1)S(1)} %collective-permute-done.9.refs_3_, ...), custom_call_target="tpu_custom_call" | custom-call | flops 1000000 | bytes 1049600 | tf_op jit(solution)/shard_map/root/pallas_call | solution.py:23
  85.5 0.0 copy-start.1
  85.6 0.6 rows.3.refs_0_
  86.1 0.1 collective-permute-start.14
  86.2 0.5 collective-permute-start.13
  86.7 3.2 %collective-permute-done.14.refs_2_ = bf16[64,1024]{1,0:T(8,128)(2,1)S(1)} collective-permute-done((bf16[64,1024]{1,0:T(8,128)(2,1)S(1)}, bf16[64,1024]{1,0:T(8,128)(2,1)S(1)}, u32[]{:S(2)}, u32[]{:S(2)}) %collective-permute-start.14) | collective-permute-done | bytes 131104 | tf_op jit(solution)/shard_map/ppermute | solution.py:213
  89.9 1.3 collective-permute-done.13.refs_1_
  91.3 0.5 collective-permute-start.17
  91.8 2.6 %collective-permute-start.16 = (bf16[64,1024]{1,0:T(8,128)(2,1)S(1)}, bf16[64,1024]{1,0:T(8,128)(2,1)S(1)}, u32[]{:S(2)}, u32[]{:S(2)}) collective-permute-start(bf16[64,1024]{1,0:T(8,128)(2,1)S(1)} %sum.7.refs_0_), channel_id=1, source_target_pairs={{0,2},{1,3},{2,0},{3,1},{4,6},{5,7},{6,4},{7,5},{8,10},{9,11},{10,... | collective-permute-start | bytes 393224 | tf_op jit(solution)/shard_map/ppermute | solution.py:213
  94.4 1.1 collective-permute-start.15
  95.5 1.8 %tile.4.state = f32[512,1024]{1,0:T(8,128)S(1)} custom-call(f32[512,1024]{1,0:T(8,128)S(1)} %copy-done.1, bf16[256,1024]{1,0:T(8,128)(2,1)S(1)} %root.4.transformed.refs_4_, f32[1,1]{1,0:T(1,128)} %get-tuple-element.55.factor), custom_call_target="tpu_custom_call" | custom-call | flops 536870912 | bytes 4718596 | tf_op jit(solution)/shard_map/tile/pallas_call | solution.py:23
  97.3 2.0 %collective-permute-done.17.refs_3_ = bf16[64,1024]{1,0:T(8,128)(2,1)S(1)} collective-permute-done((bf16[64,1024]{1,0:T(8,128)(2,1)S(1)}, bf16[64,1024]{1,0:T(8,128)(2,1)S(1)}, u32[]{:S(2)}, u32[]{:S(2)}) %collective-permute-start.17) | collective-permute-done | bytes 131104 | tf_op jit(solution)/shard_map/ppermute | solution.py:213
  99.4 0.6 collective-permute-done.15.refs_1_
  100.0 8.2 %root.5.transformed.refs_6_ = bf16[256,1024]{1,0:T(8,128)(2,1)S(1)} custom-call(bf16[64,1024]{1,0:T(8,128)(2,1)S(1)} %sum.7.refs_0_, bf16[64,1024]{1,0:T(8,128)(2,1)S(1)} %collective-permute-done.15.refs_1_, bf16[64,1024]{1,0:T(8,128)(2,1)S(1)} %collective-permute-done.16.refs_2_, bf16[64,1024]{1,0:T(8,128)(2,1)S(1)} %collective-permute-done.17.refs_3_, ...), custom_call_target="tpu_custom_call" | custom-call | flops 1000000 | bytes 1049600 | tf_op jit(solution)/shard_map/root/pallas_call | solution.py:23
  108.1 1.1 rows.4.refs_0_
  109.3 1.0 collective-permute-start.19
  110.3 1.1 collective-permute-start.18
  111.4 2.9 %collective-permute-done.19.refs_2_ = bf16[64,1024]{1,0:T(8,128)(2,1)S(1)} collective-permute-done((bf16[64,1024]{1,0:T(8,128)(2,1)S(1)}, bf16[64,1024]{1,0:T(8,128)(2,1)S(1)}, u32[]{:S(2)}, u32[]{:S(2)}) %collective-permute-start.19) | collective-permute-done | bytes 131104 | tf_op jit(solution)/shard_map/ppermute | solution.py:213
  114.3 1.4 collective-permute-done.18.refs_1_
  115.8 1.0 collective-permute-start.22
  116.7 3.2 %collective-permute-start.21 = (bf16[64,1024]{1,0:T(8,128)(2,1)S(1)}, bf16[64,1024]{1,0:T(8,128)(2,1)S(1)}, u32[]{:S(2)}, u32[]{:S(2)}) collective-permute-start(bf16[64,1024]{1,0:T(8,128)(2,1)S(1)} %sum.8.refs_0_), channel_id=1, source_target_pairs={{0,2},{1,3},{2,0},{3,1},{4,6},{5,7},{6,4},{7,5},{8,10},{9,11},{10,... | collective-permute-start | bytes 393224 | tf_op jit(solution)/shard_map/ppermute | solution.py:213
  120.0 1.2 collective-permute-start.20
  121.2 1.9 %tile.5.state = f32[512,1024]{1,0:T(8,128)S(1)} custom-call(f32[512,1024]{1,0:T(8,128)S(1)} %tile.4.state, bf16[256,1024]{1,0:T(8,128)(2,1)S(1)} %root.5.transformed.refs_6_, f32[1,1]{1,0:T(1,128)} %get-tuple-element.63.factor), custom_call_target="tpu_custom_call" | custom-call | flops 536870912 | bytes 4718596 | tf_op jit(solution)/shard_map/tile/pallas_call | solution.py:23
  123.1 0.3 collective-permute-done.22.refs_3_
  123.4 1.7 collective-permute-done.21.refs_2_
  125.1 0.1 collective-permute-done.20.refs_1_
  125.1 8.2 %root.6.transformed.refs_8_ = bf16[256,1024]{1,0:T(8,128)(2,1)S(1)} custom-call(bf16[64,1024]{1,0:T(8,128)(2,1)S(1)} %sum.8.refs_0_, bf16[64,1024]{1,0:T(8,128)(2,1)S(1)} %collective-permute-done.20.refs_1_, bf16[64,1024]{1,0:T(8,128)(2,1)S(1)} %collective-permute-done.21.refs_2_, bf16[64,1024]{1,0:T(8,128)(2,1)S(1)} %collective-permute-done.22.refs_3_, ...), custom_call_target="tpu_custom_call" | custom-call | flops 1000000 | bytes 1049600 | tf_op jit(solution)/shard_map/root/pallas_call | solution.py:23
  133.3 1.6 rows.5.refs_0_
  134.9 2.7 %collective-permute-start.24 = (bf16[64,1024]{1,0:T(8,128)(2,1)S(1)}, bf16[64,1024]{1,0:T(8,128)(2,1)S(1)}, u32[]{:S(2)}, u32[]{:S(2)}) collective-permute-start(bf16[64,1024]{1,0:T(8,128)(2,1)S(1)} %rows.5.refs_0_), channel_id=1, source_target_pairs={{8,16},{9,17},{10,18},{11,19},{12,8},{13,9},{14,10},{15,11},{16,12... | collective-permute-start | bytes 393224 | tf_op jit(solution)/shard_map/ppermute | solution.py:213
  137.6 2.7 %collective-permute-start.23 = (bf16[64,1024]{1,0:T(8,128)(2,1)S(1)}, bf16[64,1024]{1,0:T(8,128)(2,1)S(1)}, u32[]{:S(2)}, u32[]{:S(2)}) collective-permute-start(bf16[64,1024]{1,0:T(8,128)(2,1)S(1)} %rows.5.refs_0_), channel_id=1, source_target_pairs={{8,12},{9,13},{10,14},{11,15},{12,16},{13,17},{14,18},{15,19},{16,... | collective-permute-start | bytes 393224 | tf_op jit(solution)/shard_map/ppermute | solution.py:213
  140.3 2.9 %collective-permute-done.24.refs_2_ = bf16[64,1024]{1,0:T(8,128)(2,1)S(1)} collective-permute-done((bf16[64,1024]{1,0:T(8,128)(2,1)S(1)}, bf16[64,1024]{1,0:T(8,128)(2,1)S(1)}, u32[]{:S(2)}, u32[]{:S(2)}) %collective-permute-start.24) | collective-permute-done | bytes 131104 | tf_op jit(solution)/shard_map/ppermute | solution.py:213
  143.3 2.1 %collective-permute-done.23.refs_1_ = bf16[64,1024]{1,0:T(8,128)(2,1)S(1)} collective-permute-done((bf16[64,1024]{1,0:T(8,128)(2,1)S(1)}, bf16[64,1024]{1,0:T(8,128)(2,1)S(1)}, u32[]{:S(2)}, u32[]{:S(2)}) %collective-permute-start.23) | collective-permute-done | bytes 131104 | tf_op jit(solution)/shard_map/ppermute | solution.py:213
  145.4 0.6 collective-permute-start.27
  146.0 3.0 %collective-permute-start.26 = (bf16[64,1024]{1,0:T(8,128)(2,1)S(1)}, bf16[64,1024]{1,0:T(8,128)(2,1)S(1)}, u32[]{:S(2)}, u32[]{:S(2)}) collective-permute-start(bf16[64,1024]{1,0:T(8,128)(2,1)S(1)} %sum.9.refs_0_), channel_id=1, source_target_pairs={{0,2},{1,3},{2,0},{3,1},{4,6},{5,7},{6,4},{7,5},{8,10},{9,11},{10,... | collective-permute-start | bytes 393224 | tf_op jit(solution)/shard_map/ppermute | solution.py:213
  149.0 0.7 collective-permute-start.25
  149.7 1.9 %tile.6.state = f32[512,1024]{1,0:T(8,128)S(1)} custom-call(f32[512,1024]{1,0:T(8,128)S(1)} %tile.5.state, bf16[256,1024]{1,0:T(8,128)(2,1)S(1)} %root.6.transformed.refs_8_, f32[1,1]{1,0:T(1,128)} %get-tuple-element.68.factor), custom_call_target="tpu_custom_call" | custom-call | flops 536870912 | bytes 4718596 | tf_op jit(solution)/shard_map/tile/pallas_call | solution.py:23
  151.6 0.1 collective-permute-done.27.refs_3_
  151.6 1.7 %collective-permute-done.26.refs_2_ = bf16[64,1024]{1,0:T(8,128)(2,1)S(1)} collective-permute-done((bf16[64,1024]{1,0:T(8,128)(2,1)S(1)}, bf16[64,1024]{1,0:T(8,128)(2,1)S(1)}, u32[]{:S(2)}, u32[]{:S(2)}) %collective-permute-start.26) | collective-permute-done | bytes 131104 | tf_op jit(solution)/shard_map/ppermute | solution.py:213
  153.3 0.6 collective-permute-done.25.refs_1_
  153.9 8.2 %root.7.transformed = bf16[256,1024]{1,0:T(8,128)(2,1)S(1)} custom-call(bf16[64,1024]{1,0:T(8,128)(2,1)S(1)} %sum.9.refs_0_, bf16[64,1024]{1,0:T(8,128)(2,1)S(1)} %collective-permute-done.25.refs_1_, bf16[64,1024]{1,0:T(8,128)(2,1)S(1)} %collective-permute-done.26.refs_2_, bf16[64,1024]{1,0:T(8,128)(2,1)S(1)} %collective-permute-done.27.refs_3_, ...), custom_call_target="tpu_custom_call" | custom-call | flops 1000000 | bytes 1049600 | tf_op jit(solution)/shard_map/root/pallas_call | solution.py:23
  162.1 3.2 %tile.7 = f32[512,1024]{1,0:T(8,128)} custom-call(f32[512,1024]{1,0:T(8,128)S(1)} %tile.6.state, bf16[256,1024]{1,0:T(8,128)(2,1)S(1)} %root.7.transformed, f32[1,1]{1,0:T(1,128)} %get-tuple-element.74.factor), custom_call_target="tpu_custom_call" | custom-call | flops 536870912 | bytes 4718596 | tf_op jit(solution)/shard_map/tile/pallas_call | solution.py:23
  (26 shorter events, 0.2 us)
Async XLA Ops:
  0.1 1.6 copy-start
  1.7 0.8 copy-start.2
  4.2 10.6 %collective-permute-start.2 = (bf16[64,1024]{1,0:T(8,128)(2,1)S(1)}, bf16[64,1024]{1,0:T(8,128)(2,1)S(1)}, u32[]{:S(2)}, u32[]{:S(2)}) collective-permute-start(bf16[64,1024]{1,0:T(8,128)(2,1)S(1)} %get-tuple-element.50), channel_id=1, source_target_pairs={{0,1},{1,2},{2,3},{3,0},{4,5},{5,6},{6,7},{7,4},{8,9},{9,10},{10,1... | collective-permute-start | bytes 393224 | tf_op jit(solution)/shard_map/ppermute | solution.py:213
  6.5 8.3 %collective-permute-start.3 = (bf16[64,1024]{1,0:T(8,128)(2,1)S(1)}, bf16[64,1024]{1,0:T(8,128)(2,1)S(1)}, u32[]{:S(2)}, u32[]{:S(2)}) collective-permute-start(bf16[64,1024]{1,0:T(8,128)(2,1)S(1)} %get-tuple-element.51), channel_id=1, source_target_pairs={{0,2},{1,3},{2,0},{3,1},{4,6},{5,7},{6,4},{7,5},{8,10},{9,11},{10,... | collective-permute-start | bytes 393224 | tf_op jit(solution)/shard_map/ppermute | solution.py:213
  7.2 28.0 %copy-start.4 = (f32[1,256]{1,0:T(1,128)S(1)}, f32[1,256]{1,0:T(1,128)}, u32[]{:S(2)}) copy-start(f32[1,256]{1,0:T(1,128)} %own.1) | copy-start | bytes 3076
  7.2 64.3 %copy-start.5 = (s32[64,3,4]{0,2,1:T(4,128)S(1)}, s32[64,3,4]{0,2,1:T(4,128)}, u32[]{:S(2)}) copy-start(s32[64,3,4]{0,2,1:T(4,128)} %param.7) | copy-start | bytes 9220
  7.2 64.4 %copy-start.3 = (s32[64,256]{1,0:T(8,128)S(1)}, s32[64,256]{1,0:T(8,128)}, u32[]{:S(2)}) copy-start(s32[64,256]{1,0:T(8,128)} %obs.5) | copy-start | bytes 196612
  7.2 7.6 %collective-permute-start.4 = (bf16[64,1024]{1,0:T(8,128)(2,1)S(1)}, bf16[64,1024]{1,0:T(8,128)(2,1)S(1)}, u32[]{:S(2)}, u32[]{:S(2)}) collective-permute-start(bf16[64,1024]{1,0:T(8,128)(2,1)S(1)} %get-tuple-element.52), channel_id=1, source_target_pairs={{0,3},{1,0},{2,1},{3,2},{4,7},{5,4},{6,5},{7,6},{8,11},{9,8},{10,9... | collective-permute-start | bytes 393224 | tf_op jit(solution)/shard_map/ppermute | solution.py:213
  14.8 70.7 %collective-permute-start.10 = (f32[192,1024]{1,0:T(8,128)}, f32[192,1024]{1,0:T(8,128)S(1)}, u32[]{:S(2)}, u32[]{:S(2)}) collective-permute-start(f32[192,1024]{1,0:T(8,128)} %get-tuple-element.58), channel_id=1, source_target_pairs={{0,1},{1,2},{2,3},{3,0},{4,5},{5,6},{6,7},{7,4},{8,9},{9,10},{10,1... | collective-permute-start | bytes 2359304 | tf_op jit(solution)/shard_map/ppermute | solution.py:213
  17.8 67.7 %collective-permute-start.11 = (f32[192,1024]{1,0:T(8,128)}, f32[192,1024]{1,0:T(8,128)S(1)}, u32[]{:S(2)}, u32[]{:S(2)}) collective-permute-start(f32[192,1024]{1,0:T(8,128)} %get-tuple-element.59), channel_id=1, source_target_pairs={{0,2},{1,3},{2,0},{3,1},{4,6},{5,7},{6,4},{7,5},{8,10},{9,11},{10,... | collective-permute-start | bytes 2359304 | tf_op jit(solution)/shard_map/ppermute | solution.py:213
  19.5 66.1 %collective-permute-start.12 = (f32[192,1024]{1,0:T(8,128)}, f32[192,1024]{1,0:T(8,128)S(1)}, u32[]{:S(2)}, u32[]{:S(2)}) collective-permute-start(f32[192,1024]{1,0:T(8,128)} %get-tuple-element.60), channel_id=1, source_target_pairs={{0,3},{1,0},{2,1},{3,2},{4,7},{5,4},{6,5},{7,6},{8,11},{9,8},{10,9... | collective-permute-start | bytes 2359304 | tf_op jit(solution)/shard_map/ppermute | solution.py:213
  19.5 9.2 %collective-permute-start.6 = (bf16[64,1024]{1,0:T(8,128)(2,1)S(1)}, bf16[64,1024]{1,0:T(8,128)(2,1)S(1)}, u32[]{:S(2)}, u32[]{:S(2)}) collective-permute-start(bf16[64,1024]{1,0:T(8,128)(2,1)S(1)} %sum.5.refs_0_), channel_id=1, source_target_pairs={{252,4},{253,5},{254,6},{255,7},{0,252},{1,253},{2,254},{3,255},{4... | collective-permute-start | bytes 393224 | tf_op jit(solution)/shard_map/ppermute | solution.py:213
  25.3 7.7 %collective-permute-start.5 = (bf16[64,1024]{1,0:T(8,128)(2,1)S(1)}, bf16[64,1024]{1,0:T(8,128)(2,1)S(1)}, u32[]{:S(2)}, u32[]{:S(2)}) collective-permute-start(bf16[64,1024]{1,0:T(8,128)(2,1)S(1)} %sum.5.refs_0_), channel_id=1, source_target_pairs={{252,0},{253,1},{254,2},{255,3},{0,4},{1,5},{2,6},{3,7},{4,252},{5... | collective-permute-start | bytes 393224 | tf_op jit(solution)/shard_map/ppermute | solution.py:213
  33.1 38.2 %collective-permute-start.9 = (bf16[64,1024]{1,0:T(8,128)(2,1)S(1)}, bf16[64,1024]{1,0:T(8,128)(2,1)S(1)}, u32[]{:S(2)}, u32[]{:S(2)}) collective-permute-start(bf16[64,1024]{1,0:T(8,128)(2,1)S(1)} %sum.6.refs_0_), channel_id=1, source_target_pairs={{0,3},{1,0},{2,1},{3,2},{4,7},{5,4},{6,5},{7,6},{8,11},{9,8},{10,9... | collective-permute-start | bytes 393224 | tf_op jit(solution)/shard_map/ppermute | solution.py:213
  35.2 6.3 %collective-permute-start = (f32[1,256]{1,0:T(1,128)S(1)}, f32[1,256]{1,0:T(1,128)S(1)}, u32[]{:S(2)}, u32[]{:S(2)}) collective-permute-start(f32[1,256]{1,0:T(1,128)S(1)} %copy-done.4), channel_id=1, source_target_pairs={{0,4},{1,5},{2,6},{3,7},{4,8},{5,9},{6,10},{7,11},{8,12},{9,13},{1... | collective-permute-start | bytes 3080 | tf_op jit(solution)/shard_map/ppermute | solution.py:213
  41.5 26.7 %collective-permute-start.1 = (f32[1,256]{1,0:T(1,128)S(1)}, f32[1,256]{1,0:T(1,128)S(1)}, u32[]{:S(2)}, u32[]{:S(2)}) collective-permute-start(f32[1,256]{1,0:T(1,128)S(1)} %copy-done.4), channel_id=1, source_target_pairs={{0,252},{1,253},{2,254},{3,255},{4,0},{5,1},{6,2},{7,3},{8,4},{9,5... | collective-permute-start | bytes 3080 | tf_op jit(solution)/shard_map/ppermute | solution.py:213
  68.2 6.6 %collective-permute-start.8 = (bf16[64,1024]{1,0:T(8,128)(2,1)S(1)}, bf16[64,1024]{1,0:T(8,128)(2,1)}, u32[]{:S(2)}, u32[]{:S(2)}) collective-permute-start(bf16[64,1024]{1,0:T(8,128)(2,1)S(1)} %sum.6.refs_0_), channel_id=1, source_target_pairs={{0,2},{1,3},{2,0},{3,1},{4,6},{5,7},{6,4},{7,5},{8,10},{9,11},{10,... | collective-permute-start | bytes 393224 | tf_op jit(solution)/shard_map/ppermute | solution.py:213
  71.3 5.1 %collective-permute-start.7 = (bf16[64,1024]{1,0:T(8,128)(2,1)S(1)}, bf16[64,1024]{1,0:T(8,128)(2,1)}, u32[]{:S(2)}, u32[]{:S(2)}) collective-permute-start(bf16[64,1024]{1,0:T(8,128)(2,1)S(1)} %sum.6.refs_0_), channel_id=1, source_target_pairs={{0,1},{1,2},{2,3},{3,0},{4,5},{5,6},{6,7},{7,4},{8,9},{9,10},{10,1... | collective-permute-start | bytes 393224 | tf_op jit(solution)/shard_map/ppermute | solution.py:213
  85.5 10.0 %copy-start.1 = (f32[512,1024]{1,0:T(8,128)S(1)}, f32[512,1024]{1,0:T(8,128)}, u32[]{:S(2)}) copy-start(f32[512,1024]{1,0:T(8,128)} %state.4) | copy-start | bytes 6291460
  86.1 3.8 %collective-permute-start.14 = (bf16[64,1024]{1,0:T(8,128)(2,1)S(1)}, bf16[64,1024]{1,0:T(8,128)(2,1)S(1)}, u32[]{:S(2)}, u32[]{:S(2)}) collective-permute-start(bf16[64,1024]{1,0:T(8,128)(2,1)S(1)} %rows.3.refs_0_), channel_id=1, source_target_pairs={{0,8},{1,9},{2,10},{3,11},{4,0},{5,1},{6,2},{7,3},{8,4},{9,5},{10,... | collective-permute-start | bytes 393224 | tf_op jit(solution)/shard_map/ppermute | solution.py:213
  86.2 5.0 %collective-permute-start.13 = (bf16[64,1024]{1,0:T(8,128)(2,1)S(1)}, bf16[64,1024]{1,0:T(8,128)(2,1)S(1)}, u32[]{:S(2)}, u32[]{:S(2)}) collective-permute-start(bf16[64,1024]{1,0:T(8,128)(2,1)S(1)} %rows.3.refs_0_), channel_id=1, source_target_pairs={{0,4},{1,5},{2,6},{3,7},{4,8},{5,9},{6,10},{7,11},{8,0},{9,1},{10,... | collective-permute-start | bytes 393224 | tf_op jit(solution)/shard_map/ppermute | solution.py:213
  91.3 8.1 %collective-permute-start.17 = (bf16[64,1024]{1,0:T(8,128)(2,1)S(1)}, bf16[64,1024]{1,0:T(8,128)(2,1)S(1)}, u32[]{:S(2)}, u32[]{:S(2)}) collective-permute-start(bf16[64,1024]{1,0:T(8,128)(2,1)S(1)} %sum.7.refs_0_), channel_id=1, source_target_pairs={{0,3},{1,0},{2,1},{3,2},{4,7},{5,4},{6,5},{7,6},{8,11},{9,8},{10,9... | collective-permute-start | bytes 393224 | tf_op jit(solution)/shard_map/ppermute | solution.py:213
  91.8 7.6 %collective-permute-start.16 = (bf16[64,1024]{1,0:T(8,128)(2,1)S(1)}, bf16[64,1024]{1,0:T(8,128)(2,1)S(1)}, u32[]{:S(2)}, u32[]{:S(2)}) collective-permute-start(bf16[64,1024]{1,0:T(8,128)(2,1)S(1)} %sum.7.refs_0_), channel_id=1, source_target_pairs={{0,2},{1,3},{2,0},{3,1},{4,6},{5,7},{6,4},{7,5},{8,10},{9,11},{10,... | collective-permute-start | bytes 393224 | tf_op jit(solution)/shard_map/ppermute | solution.py:213
  94.4 5.6 %collective-permute-start.15 = (bf16[64,1024]{1,0:T(8,128)(2,1)S(1)}, bf16[64,1024]{1,0:T(8,128)(2,1)S(1)}, u32[]{:S(2)}, u32[]{:S(2)}) collective-permute-start(bf16[64,1024]{1,0:T(8,128)(2,1)S(1)} %sum.7.refs_0_), channel_id=1, source_target_pairs={{0,1},{1,2},{2,3},{3,0},{4,5},{5,6},{6,7},{7,4},{8,9},{9,10},{10,1... | collective-permute-start | bytes 393224 | tf_op jit(solution)/shard_map/ppermute | solution.py:213
  109.3 5.0 %collective-permute-start.19 = (bf16[64,1024]{1,0:T(8,128)(2,1)S(1)}, bf16[64,1024]{1,0:T(8,128)(2,1)S(1)}, u32[]{:S(2)}, u32[]{:S(2)}) collective-permute-start(bf16[64,1024]{1,0:T(8,128)(2,1)S(1)} %rows.4.refs_0_), channel_id=1, source_target_pairs={{4,12},{5,13},{6,14},{7,15},{8,4},{9,5},{10,6},{11,7},{12,8},{13,9... | collective-permute-start | bytes 393224 | tf_op jit(solution)/shard_map/ppermute | solution.py:213
  110.3 5.5 %collective-permute-start.18 = (bf16[64,1024]{1,0:T(8,128)(2,1)S(1)}, bf16[64,1024]{1,0:T(8,128)(2,1)S(1)}, u32[]{:S(2)}, u32[]{:S(2)}) collective-permute-start(bf16[64,1024]{1,0:T(8,128)(2,1)S(1)} %rows.4.refs_0_), channel_id=1, source_target_pairs={{4,8},{5,9},{6,10},{7,11},{8,12},{9,13},{10,14},{11,15},{12,4},{13... | collective-permute-start | bytes 393224 | tf_op jit(solution)/shard_map/ppermute | solution.py:213
  115.8 7.7 %collective-permute-start.22 = (bf16[64,1024]{1,0:T(8,128)(2,1)S(1)}, bf16[64,1024]{1,0:T(8,128)(2,1)S(1)}, u32[]{:S(2)}, u32[]{:S(2)}) collective-permute-start(bf16[64,1024]{1,0:T(8,128)(2,1)S(1)} %sum.8.refs_0_), channel_id=1, source_target_pairs={{0,3},{1,0},{2,1},{3,2},{4,7},{5,4},{6,5},{7,6},{8,11},{9,8},{10,9... | collective-permute-start | bytes 393224 | tf_op jit(solution)/shard_map/ppermute | solution.py:213
  116.7 8.3 %collective-permute-start.21 = (bf16[64,1024]{1,0:T(8,128)(2,1)S(1)}, bf16[64,1024]{1,0:T(8,128)(2,1)S(1)}, u32[]{:S(2)}, u32[]{:S(2)}) collective-permute-start(bf16[64,1024]{1,0:T(8,128)(2,1)S(1)} %sum.8.refs_0_), channel_id=1, source_target_pairs={{0,2},{1,3},{2,0},{3,1},{4,6},{5,7},{6,4},{7,5},{8,10},{9,11},{10,... | collective-permute-start | bytes 393224 | tf_op jit(solution)/shard_map/ppermute | solution.py:213
  120.0 5.2 %collective-permute-start.20 = (bf16[64,1024]{1,0:T(8,128)(2,1)S(1)}, bf16[64,1024]{1,0:T(8,128)(2,1)S(1)}, u32[]{:S(2)}, u32[]{:S(2)}) collective-permute-start(bf16[64,1024]{1,0:T(8,128)(2,1)S(1)} %sum.8.refs_0_), channel_id=1, source_target_pairs={{0,1},{1,2},{2,3},{3,0},{4,5},{5,6},{6,7},{7,4},{8,9},{9,10},{10,1... | collective-permute-start | bytes 393224 | tf_op jit(solution)/shard_map/ppermute | solution.py:213
  134.9 8.4 %collective-permute-start.24 = (bf16[64,1024]{1,0:T(8,128)(2,1)S(1)}, bf16[64,1024]{1,0:T(8,128)(2,1)S(1)}, u32[]{:S(2)}, u32[]{:S(2)}) collective-permute-start(bf16[64,1024]{1,0:T(8,128)(2,1)S(1)} %rows.5.refs_0_), channel_id=1, source_target_pairs={{8,16},{9,17},{10,18},{11,19},{12,8},{13,9},{14,10},{15,11},{16,12... | collective-permute-start | bytes 393224 | tf_op jit(solution)/shard_map/ppermute | solution.py:213
  137.6 7.7 %collective-permute-start.23 = (bf16[64,1024]{1,0:T(8,128)(2,1)S(1)}, bf16[64,1024]{1,0:T(8,128)(2,1)S(1)}, u32[]{:S(2)}, u32[]{:S(2)}) collective-permute-start(bf16[64,1024]{1,0:T(8,128)(2,1)S(1)} %rows.5.refs_0_), channel_id=1, source_target_pairs={{8,12},{9,13},{10,14},{11,15},{12,16},{13,17},{14,18},{15,19},{16,... | collective-permute-start | bytes 393224 | tf_op jit(solution)/shard_map/ppermute | solution.py:213
  145.4 6.3 %collective-permute-start.27 = (bf16[64,1024]{1,0:T(8,128)(2,1)S(1)}, bf16[64,1024]{1,0:T(8,128)(2,1)S(1)}, u32[]{:S(2)}, u32[]{:S(2)}) collective-permute-start(bf16[64,1024]{1,0:T(8,128)(2,1)S(1)} %sum.9.refs_0_), channel_id=1, source_target_pairs={{0,3},{1,0},{2,1},{3,2},{4,7},{5,4},{6,5},{7,6},{8,11},{9,8},{10,9... | collective-permute-start | bytes 393224 | tf_op jit(solution)/shard_map/ppermute | solution.py:213
  146.0 7.4 %collective-permute-start.26 = (bf16[64,1024]{1,0:T(8,128)(2,1)S(1)}, bf16[64,1024]{1,0:T(8,128)(2,1)S(1)}, u32[]{:S(2)}, u32[]{:S(2)}) collective-permute-start(bf16[64,1024]{1,0:T(8,128)(2,1)S(1)} %sum.9.refs_0_), channel_id=1, source_target_pairs={{0,2},{1,3},{2,0},{3,1},{4,6},{5,7},{6,4},{7,5},{8,10},{9,11},{10,... | collective-permute-start | bytes 393224 | tf_op jit(solution)/shard_map/ppermute | solution.py:213
  149.0 5.0 %collective-permute-start.25 = (bf16[64,1024]{1,0:T(8,128)(2,1)S(1)}, bf16[64,1024]{1,0:T(8,128)(2,1)S(1)}, u32[]{:S(2)}, u32[]{:S(2)}) collective-permute-start(bf16[64,1024]{1,0:T(8,128)(2,1)S(1)} %sum.9.refs_0_), channel_id=1, source_target_pairs={{0,1},{1,2},{2,3},{3,0},{4,5},{5,6},{6,7},{7,4},{8,9},{9,10},{10,1... | collective-permute-start | bytes 393224 | tf_op jit(solution)/shard_map/ppermute | solution.py:213
